TPU v7x, 32 devices: a whole 2x2x4 slice. The times are simulated.
32 devices in a mesh: fsdp: 16 (over z, y, core), tp: 2 (over x).
Axes of the slice: x: 2, y: 2, z: 4, core: 2. Of those that a mesh axis runs over, the one named last changes fastest.
Arguments:
- tokens: bfloat16 [16, 1024, 1152], P('fsdp', 'tp'), may hold values from -6 to 6
- condition: bfloat16 [16, 1152], P('fsdp'), may hold values from -3 to 3
- mod_weight: bfloat16 [1152, 6912], P('tp', 'fsdp'), may hold values from -0.088388348 to 0.088388348
- mod_bias: bfloat16 [6912], P('fsdp'), may hold values from -1.5 to 1.5
- qkv_weight: bfloat16 [1152, 3, 1152], P('fsdp', None, 'tp'), may hold values from -0.088388348 to 0.088388348
- qv_bias: bfloat16 [2, 1152], P(None, 'fsdp'), may hold values from -2 to 2
- out_weight: bfloat16 [1152, 1152], P('tp', 'fsdp'), may hold values from -0.75 to 0.75
- out_bias: bfloat16 [1152], P('fsdp'), may hold values from -3 to 3
- up_weight: bfloat16 [1152, 4608], P('fsdp', 'tp'), may hold values from -0.1875 to 0.1875
- up_bias: bfloat16 [4608], P('fsdp'), may hold values from -3 to 3
- down_weight: bfloat16 [4608, 1152], P('tp', 'fsdp'), may hold values from -0.09375 to 0.09375
- down_bias: bfloat16 [1152], P('fsdp'), may hold values from -3 to 3
- cotangent: bfloat16 [16, 1024, 1152], P('fsdp', 'tp'), may hold values from -6 to 6
Outputs:
- result: bfloat16 [16, 1024, 1152], P('fsdp', 'tp')
- tokens_grad: bfloat16 [16, 1024, 1152], P('fsdp', 'tp')
- condition_grad: float32 [16, 1152], P('fsdp', 'tp')
- mod_weight_grad: float32 [1152, 6912], P('tp', 'fsdp')
- mod_bias_grad: float32 [6912], P('fsdp')
- qkv_weight_grad: float32 [1152, 3, 1152], P('fsdp', None, 'tp')
- qv_bias_grad: float32 [2, 1152], P(None, 'fsdp')
- out_weight_grad: float32 [1152, 1152], P('tp', 'fsdp')
- out_bias_grad: float32 [1152], P('fsdp')
- up_weight_grad: float32 [1152, 4608], P('fsdp', 'tp')
- up_bias_grad: float32 [4608], P('fsdp')
- down_weight_grad: float32 [4608, 1152], P('tp', 'fsdp')
- down_bias_grad: float32 [1152], P('fsdp')
All inputs are finite; a program needn't handle non-finite values.
Results may differ from a plain program's by a relative error of at most 0.015.
Values may be sent and summed in bfloat16 or wider, within the bound.
A program may use at most 256 MiB of HBM per device.

v0:
```python
import math

import jax
import jax.numpy as jnp
from jax import lax
from jax.sharding import PartitionSpec as P

HEAD_DIM = 72


EPSILON = 1e-06
HIGH = lax.Precision.HIGHEST


def normalize(values):
    center = values - jnp.mean(values, axis=-1, keepdims=True)
    variance = jnp.mean(center * center, axis=-1, keepdims=True)
    inverse = lax.rsqrt(variance + EPSILON)
    return (center * inverse, inverse)


def norm_back(grad_norm, normed, inverse):
    first_mean = jnp.mean(grad_norm, axis=-1, keepdims=True)
    second_mean = jnp.mean(grad_norm * normed, axis=-1, keepdims=True)
    return inverse * (grad_norm - first_mean - normed * second_mean)


def inner_rows(left, right):
    return lax.dot_general(
        left, right, (((0,), (0,)), ((), ())), preferred_element_type=jnp.float32
    )


def outer_cols(left, right):
    return lax.dot_general(
        left, right, (((1,), (1,)), ((), ())), preferred_element_type=jnp.float32
    )


def gelu_tanh(values):
    return jax.nn.gelu(values, approximate=True)


def to_heads(flat, head_count):
    return flat.reshape(flat.shape[0], head_count, HEAD_DIM).transpose(1, 0, 2)


def from_heads(stacked):
    return stacked.transpose(1, 0, 2).reshape(stacked.shape[1], stacked.shape[0] * HEAD_DIM)


def shards(
    tokens,
    condition,
    mod_weight,
    mod_bias,
    qkv_weight,
    qv_bias,
    out_weight,
    out_bias,
    up_weight,
    up_bias,
    down_weight,
    down_bias,
    cotangent,
):
    tp_count = lax.axis_size("tp")
    tp_place = lax.axis_index("tp")
    local_rows = tokens.shape[1]
    width = tokens.shape[2]
    seq_len = local_rows * tp_count
    share = width // tp_count
    (
        mod_full,
        mod_shift,
        qkv_full,
        qv_full,
        out_full,
        out_shift,
        up_full,
        up_shift,
        down_full,
        down_shift,
    ) = (
        lax.all_gather(mod_weight, "fsdp", axis=1, tiled=True),
        lax.all_gather(mod_bias, "fsdp", axis=0, tiled=True),
        lax.all_gather(qkv_weight, "fsdp", axis=0, tiled=True),
        lax.all_gather(qv_bias, "fsdp", axis=1, tiled=True),
        lax.all_gather(out_weight, "fsdp", axis=1, tiled=True),
        lax.all_gather(out_bias, "fsdp", axis=0, tiled=True),
        lax.all_gather(up_weight, "fsdp", axis=0, tiled=True),
        lax.all_gather(up_bias, "fsdp", axis=0, tiled=True),
        lax.all_gather(down_weight, "fsdp", axis=1, tiled=True),
        lax.all_gather(down_bias, "fsdp", axis=0, tiled=True),
    )
    head_cols = qkv_full.shape[2]
    head_count = head_cols // HEAD_DIM
    hidden_cols = up_full.shape[1]
    cond_row = condition[0].astype(jnp.float32)
    cond_part = lax.dynamic_slice_in_dim(cond_row, tp_place * share, share)
    silu_part, silu_pull = jax.vjp(jax.nn.silu, cond_part)
    silu_low = silu_part.astype(jnp.bfloat16)
    partial_mod = jnp.dot(silu_low[None, :], mod_full, preferred_element_type=jnp.float32)[0]
    modulation = lax.psum(partial_mod, "tp") + mod_shift.astype(jnp.float32)
    pieces = modulation.reshape(6, width)
    shift_one = pieces[0]
    scale_one = pieces[1]
    gate_one = pieces[2]
    shift_two = pieces[3]
    scale_two = pieces[4]
    gate_two = pieces[5]
    rows_in = tokens[0].astype(jnp.float32)
    normed_one, inverse_one = normalize(rows_in)
    hidden_one = lax.all_gather(
        (normed_one * (1.0 + scale_one) + shift_one).astype(jnp.bfloat16), "tp", axis=0, tiled=True
    )
    qkv_matrix = qkv_full.reshape(width, 3 * head_cols)
    projected = jnp.dot(hidden_one, qkv_matrix, preferred_element_type=jnp.float32).reshape(
        seq_len, 3, head_cols
    )
    qv_local = lax.dynamic_slice_in_dim(
        qv_full.astype(jnp.float32), tp_place * head_cols, head_cols, 1
    )
    queries = to_heads((projected[:, 0] + qv_local[0]).astype(jnp.bfloat16), head_count)
    keys_all = to_heads(projected[:, 1].astype(jnp.bfloat16), head_count)
    values_all = to_heads((projected[:, 2] + qv_local[1]).astype(jnp.bfloat16), head_count)
    block = min(512, seq_len)
    block_count = seq_len // block
    scaling = 1.0 / math.sqrt(HEAD_DIM)
    query_blocks = queries.reshape(head_count, block_count, block, HEAD_DIM).transpose(1, 0, 2, 3)

    def attend(query_block):
        scores = (
            jnp.einsum("hqd,hkd->hqk", query_block, keys_all, preferred_element_type=jnp.float32)
            * scaling
        )
        highest = jnp.max(scores, axis=-1, keepdims=True)
        raised = jnp.exp(scores - highest)
        totals = jnp.sum(raised, axis=-1, keepdims=True)
        weights = (raised / totals).astype(jnp.bfloat16)
        output = jnp.einsum("hqk,hkd->hqd", weights, values_all, preferred_element_type=jnp.float32)
        return (output, (highest + jnp.log(totals))[..., 0])

    attended_blocks, log_totals = lax.map(attend, query_blocks)
    attended = attended_blocks.transpose(1, 0, 2, 3).reshape(head_count, seq_len, HEAD_DIM)
    attended_low = from_heads(attended).astype(jnp.bfloat16)
    picked = attended_low
    branch_one = lax.psum_scatter(
        jnp.dot(picked, out_full, preferred_element_type=jnp.float32),
        "tp",
        scatter_dimension=0,
        tiled=True,
    ) + out_shift.astype(jnp.float32)
    middle = rows_in + gate_one * branch_one
    normed_two, inverse_two = normalize(middle)
    hidden_two = lax.all_gather(
        (normed_two * (1.0 + scale_two) + shift_two).astype(jnp.bfloat16), "tp", axis=0, tiled=True
    )
    up_local = lax.dynamic_slice_in_dim(
        up_shift.astype(jnp.float32), tp_place * hidden_cols, hidden_cols
    )
    before = jnp.dot(hidden_two, up_full, preferred_element_type=jnp.float32) + up_local
    activated, gelu_pull = jax.vjp(gelu_tanh, before)
    activated_low = activated.astype(jnp.bfloat16)
    picked = activated_low
    branch_two = lax.psum_scatter(
        jnp.dot(picked, down_full, preferred_element_type=jnp.float32).astype(jnp.bfloat16),
        "tp",
        scatter_dimension=0,
        tiled=True,
    ).astype(jnp.float32) + down_shift.astype(jnp.float32)
    outcome = (middle + gate_two * branch_two).astype(jnp.bfloat16)
    grad_rows = cotangent[0].astype(jnp.float32)
    grad_gate_two = jnp.sum(grad_rows * branch_two, axis=0)
    grad_branch_two = lax.all_gather(
        (grad_rows * gate_two).astype(jnp.bfloat16), "tp", axis=0, tiled=True
    )
    down_bias_term = jnp.sum(grad_branch_two.astype(jnp.float32), axis=0)
    down_weight_term = inner_rows(activated_low, grad_branch_two)
    grad_before = gelu_pull(outer_cols(grad_branch_two, down_full))[0].astype(jnp.bfloat16)
    up_bias_part = jnp.sum(grad_before.astype(jnp.float32), axis=0)
    up_weight_term = inner_rows(hidden_two, grad_before)
    picked = grad_before
    grad_hidden_two = lax.psum_scatter(
        outer_cols(picked, up_full), "tp", scatter_dimension=0, tiled=True
    )
    grad_scale_two = jnp.sum(grad_hidden_two * normed_two, axis=0)
    grad_shift_two = jnp.sum(grad_hidden_two, axis=0)
    grad_middle = grad_rows + norm_back(
        grad_hidden_two * (1.0 + scale_two), normed_two, inverse_two
    )
    grad_gate_one = jnp.sum(grad_middle * branch_one, axis=0)
    grad_branch_one = lax.all_gather(
        (grad_middle * gate_one).astype(jnp.bfloat16), "tp", axis=0, tiled=True
    )
    out_bias_term = jnp.sum(grad_branch_one.astype(jnp.float32), axis=0)
    out_weight_term = inner_rows(attended_low, grad_branch_one)
    grad_attended = outer_cols(grad_branch_one, out_full).astype(jnp.bfloat16)
    grad_blocks = (
        to_heads(grad_attended, head_count)
        .reshape(head_count, block_count, block, HEAD_DIM)
        .transpose(1, 0, 2, 3)
    )

    def attend_back(carry, inputs):
        grad_keys, grad_values = carry
        query_block, log_block, grad_block = inputs
        scores = (
            jnp.einsum("hqd,hkd->hqk", query_block, keys_all, preferred_element_type=jnp.float32)
            * scaling
        )
        weights = jnp.exp(scores - log_block[..., None])
        grad_weights = jnp.einsum(
            "hqd,hkd->hqk", grad_block, values_all, preferred_element_type=jnp.float32
        )
        centered = jnp.sum(weights * grad_weights, axis=-1, keepdims=True)
        grad_scores = (weights * (grad_weights - centered)).astype(jnp.bfloat16)
        grad_query = (
            jnp.einsum("hqk,hkd->hqd", grad_scores, keys_all, preferred_element_type=jnp.float32)
            * scaling
        )
        grad_keys = (
            grad_keys
            + jnp.einsum(
                "hqk,hqd->hkd", grad_scores, query_block, preferred_element_type=jnp.float32
            )
            * scaling
        )
        grad_values = grad_values + jnp.einsum(
            "hqk,hqd->hkd",
            weights.astype(jnp.bfloat16),
            grad_block,
            preferred_element_type=jnp.float32,
        )
        return ((grad_keys, grad_values), grad_query)

    zero_heads = jnp.zeros((head_count, seq_len, HEAD_DIM), jnp.float32)
    (grad_keys, grad_values), grad_query_blocks = lax.scan(
        attend_back, (zero_heads, zero_heads), (query_blocks, log_totals, grad_blocks)
    )
    grad_queries = grad_query_blocks.transpose(1, 0, 2, 3).reshape(head_count, seq_len, HEAD_DIM)
    grad_projected = jnp.stack(
        [from_heads(grad_queries), from_heads(grad_keys), from_heads(grad_values)], axis=1
    ).astype(jnp.bfloat16)
    qv_bias_part = jnp.sum(grad_projected[:, 0::2].astype(jnp.float32), axis=0)
    grad_flat = grad_projected.reshape(seq_len, 3 * head_cols)
    qkv_weight_term = inner_rows(hidden_one, grad_flat).reshape(width, 3, head_cols)
    picked = grad_flat
    grad_hidden_one = lax.psum_scatter(
        outer_cols(picked, qkv_matrix).astype(jnp.bfloat16), "tp", scatter_dimension=0, tiled=True
    ).astype(jnp.float32)
    grad_scale_one = jnp.sum(grad_hidden_one * normed_one, axis=0)
    grad_shift_one = jnp.sum(grad_hidden_one, axis=0)
    grad_tokens = grad_middle + norm_back(
        grad_hidden_one * (1.0 + scale_one), normed_one, inverse_one
    )
    grad_mod_part = jnp.concatenate(
        [
            grad_shift_one,
            grad_scale_one,
            grad_gate_one,
            grad_shift_two,
            grad_scale_two,
            grad_gate_two,
        ]
    )
    qv_padded = lax.dynamic_update_slice_in_dim(
        jnp.zeros((2, width), jnp.float32), qv_bias_part, tp_place * head_cols, 1
    )
    up_padded = lax.dynamic_update_slice_in_dim(
        jnp.zeros((up_shift.shape[0],), jnp.float32), up_bias_part, tp_place * hidden_cols, 0
    )
    grad_mod, qv_bias_term, up_bias_term = (
        lax.psum(grad_mod_part.astype(jnp.bfloat16), "tp").astype(jnp.float32),
        lax.psum(qv_padded.astype(jnp.bfloat16), "tp").astype(jnp.float32),
        lax.psum(up_padded.astype(jnp.bfloat16), "tp").astype(jnp.float32),
    )
    grad_silu = jnp.dot(mod_full.astype(jnp.float32), grad_mod, precision=HIGH)
    cond_grad = silu_pull(grad_silu)[0][None, :]
    mod_weight_term = silu_low.astype(jnp.float32)[:, None] * grad_mod[None, :]
    (
        mod_weight_grad,
        mod_bias_grad,
        qkv_weight_grad,
        qv_bias_grad,
        out_weight_grad,
        out_bias_grad,
        up_weight_grad,
        up_bias_grad,
        down_weight_grad,
        down_bias_grad,
    ) = (
        lax.psum_scatter(mod_weight_term, "fsdp", scatter_dimension=1, tiled=True),
        lax.psum_scatter(grad_mod, "fsdp", scatter_dimension=0, tiled=True),
        lax.psum_scatter(qkv_weight_term, "fsdp", scatter_dimension=0, tiled=True),
        lax.psum_scatter(qv_bias_term, "fsdp", scatter_dimension=1, tiled=True),
        lax.psum_scatter(out_weight_term, "fsdp", scatter_dimension=1, tiled=True),
        lax.psum_scatter(out_bias_term, "fsdp", scatter_dimension=0, tiled=True),
        lax.psum_scatter(up_weight_term, "fsdp", scatter_dimension=0, tiled=True),
        lax.psum_scatter(up_bias_term, "fsdp", scatter_dimension=0, tiled=True),
        lax.psum_scatter(down_weight_term, "fsdp", scatter_dimension=1, tiled=True),
        lax.psum_scatter(down_bias_term, "fsdp", scatter_dimension=0, tiled=True),
    )
    return (
        outcome[None],
        grad_tokens.astype(jnp.bfloat16)[None],
        cond_grad,
        mod_weight_grad,
        mod_bias_grad,
        qkv_weight_grad,
        qv_bias_grad,
        out_weight_grad,
        out_bias_grad,
        up_weight_grad,
        up_bias_grad,
        down_weight_grad,
        down_bias_grad,
    )


def solution(mesh):
    return jax.shard_map(
        shards,
        mesh=mesh,
        in_specs=(
            P("fsdp", "tp", None),
            P("fsdp", None),
            P("tp", "fsdp"),
            P("fsdp"),
            P("fsdp", None, "tp"),
            P(None, "fsdp"),
            P("tp", "fsdp"),
            P("fsdp"),
            P("fsdp", "tp"),
            P("fsdp"),
            P("tp", "fsdp"),
            P("fsdp"),
            P("fsdp", "tp", None),
        ),
        out_specs=(
            P("fsdp", "tp", None),
            P("fsdp", "tp", None),
            P("fsdp", "tp"),
            P("tp", "fsdp"),
            P("fsdp"),
            P("fsdp", None, "tp"),
            P(None, "fsdp"),
            P("tp", "fsdp"),
            P("fsdp"),
            P("fsdp", "tp"),
            P("fsdp"),
            P("tp", "fsdp"),
            P("fsdp"),
        ),
        check_vma=False,
    )
```

profile of v0, /device:TPU:0, one launch (start us, length us, event | category | flops | bytes accessed | tf_op | source)
XLA Modules:
  0.0 1452.1 jit_solution(4694295346993704896)
XLA Ops:
  17.4 65.6 %all-reduce.11 = (bf16[6912]{0:T(1024)(128)(2,1)S(1)}, bf16[1152]{0:T(1024)(128)(2,1)}, bf16[4608]{0:T(1024)(128)(2,1)}, bf16[1152]{0:T(1024)(128)(2,1)}) all-reduce(bf16[6912]{0:T(1024)(128)(2,1)S(1)} %dynamic-update-slice, bf16[1152]{0:T(1024)(128)(2,1)S(1)} %dynamic-update-slice.1, ...), channel_id=1, replica_groups=mesh['fsdp'=16,'tp'=2] {'fsdp'}, use_global_device_ids=true, to_apply=%add | all-reduce | flops 13824 | bytes 55296
  85.0 6.6 all-gather.11.cloned.1.call-done
  91.6 5.9 convolution_reduce_fusion
  97.5 8.3 psum.28
  109.2 18.8 %all-gather = bf16[16,72,2]{1,2,0:T(2,128)(2,1)S(1)} all-gather(bf16[1,72,2]{1,2,0:T(2,128)(2,1)S(1)} %bitcast.228), channel_id=1, replica_groups=mesh['fsdp'=16,'tp'=2] {'fsdp'}, dimensions={0}, use_global_device_ids=true | all-gather | bytes 4896 | tf_op jit(solution)/shard_map/all_gather | solution.py:88
  128.4 15.3 %all-gather.15.cloned.1.call-done = bf16[1152,3,576]{2,0,1:T(8,128)(2,1)} async-done(((bf16[72,3,576]{2,0,1:T(8,128)(2,1)}), bf16[1152,3,576]{2,0,1:T(8,128)(2,1)}) %all-gather.15.cloned.1.call-update) | async-done | bytes 3981328 | tf_op jit(solution)/shard_map/all_gather | solution.py:87
  143.7 6.5 copy.43
  150.2 30.2 %all-gather.13.cloned.1.call-done = bf16[1024,1152]{1,0:T(8,128)(2,1)} async-done(((bf16[512,1152]{1,0:T(8,128)(2,1)}), bf16[1024,1152]{1,0:T(8,128)(2,1)}) %all-gather.13.cloned.1.call-update) | async-done | bytes 2359312 | tf_op jit(solution)/shard_map/all_gather | solution.py:114
  180.4 7.3 fusion.40
  194.1 24.2 %while.27 = (s32[]{:T(128)}, bf16[2,8,512,72]{2,3,1,0:T(8,128)(2,1)}, f32[2,8,512]{2,1,0:T(8,128)}, bf16[2,8,512,72]{2,3,1,0:T(8,128)(2,1)S(1)}, bf16[8,1024,72]...) while((s32[]{:T(128)}, bf16[2,8,512,72]{2,3,1,0:T(8,128)(2,1)}, ...), condition=%wide.region_6.7_spmd, body=%wide.region_3.6_spmd.sunk | while | flops 1245704192 | bytes 64291024 | solution.py:144
  194.1 2.5 multiply_reduce_fusion.9
  196.6 3.5 fusion.132
  200.2 4.4 fusion.133
  206.2 2.5 multiply_reduce_fusion.9
  208.7 3.5 fusion.132
  212.2 4.4 fusion.133
  218.2 2.5 copy.55
  221.8 6.1 fusion.81
  229.3 57.8 %reduce-scatter.13.cloned.1.call-done = f32[512,1152]{1,0:T(8,128)} async-done(((f32[1024,1152]{1,0:T(8,128)}), f32[512,1152]{1,0:T(8,128)}) %reduce-scatter.13.cloned.1.call-update) | async-done | bytes 2359312 | tf_op jit(solution)/shard_map/reduce_scatter | solution.py:148
  293.3 2.5 fusion.62
  297.4 48.3 %all-gather.21.cloned.1.call-done = bf16[1152,2304]{1,0:T(8,128)(2,1)} async-done(((bf16[72,2304]{1,0:T(8,128)(2,1)}), bf16[1152,2304]{1,0:T(8,128)(2,1)}) %all-gather.21.cloned.1.call-update) | async-done | bytes 5308432 | tf_op jit(solution)/shard_map/all_gather | solution.py:91
  345.7 36.9 %all-gather.19.cloned.1.call-done = bf16[1024,1152]{1,0:T(8,128)(2,1)} async-done(((bf16[512,1152]{1,0:T(8,128)(2,1)}), bf16[1024,1152]{1,0:T(8,128)(2,1)}) %all-gather.19.cloned.1.call-update) | async-done | bytes 2359312 | tf_op jit(solution)/shard_map/all_gather | solution.py:156
  382.6 11.4 fusion.82
  394.0 47.4 %all-gather.23.cloned.1.call-done = bf16[2304,1152]{0,1:T(8,128)(2,1)} async-done(((bf16[2304,72]{0,1:T(8,128)(2,1)}), bf16[2304,1152]{0,1:T(8,128)(2,1)}) %all-gather.23.cloned.1.call-update) | async-done | bytes 5308432 | tf_op jit(solution)/shard_map/all_gather | solution.py:93
  441.4 36.9 %all-gather.25.cloned.1.call-done = bf16[1024,1152]{1,0:T(8,128)(2,1)} async-done(((bf16[512,1152]{1,0:T(8,128)(2,1)}), bf16[1024,1152]{1,0:T(8,128)(2,1)}) %all-gather.25.cloned.1.call-update) | async-done | bytes 2359312 | tf_op jit(solution)/shard_map/all_gather | solution.py:175
  478.2 15.4 %convert_reduce_fusion = (bf16[2304]{0:T(1024)(128)(2,1)}, bf16[1024,2304]{1,0:T(8,128)(2,1)S(1)}) fusion(f32[1024,2304]{1,0:T(8,128)} %fusion.82, f32[2304]{0:T(1024)} %dynamic-slice_convert_fusion, bf16[1024,1152]{1,0:T(8,128)(2,1)} %all-gather.25.cloned.1.call-done, bf16[2304,1152]{0,1:T(8,128)(2,1)} %all-gather.23.cloned.1.call-done), kind=kOutput, calls=%fused_computation.50 | convolution fusion | flops 5490079744 | bytes 21837312 | tf_op jit(solution)/shard_map/dot_general | solution.py:35
  495.7 10.4 fusion.83
  506.6 13.4 convolution_convert_fusion
  521.4 44.8 %reduce-scatter.17.cloned.1.call-done = f32[512,1152]{1,0:T(8,128)} async-done(((f32[1024,1152]{1,0:T(8,128)}), f32[512,1152]{1,0:T(8,128)}) %reduce-scatter.17.cloned.1.call-update) | async-done | bytes 2359312 | tf_op jit(solution)/shard_map/reduce_scatter | solution.py:184
  566.3 3.9 multiply_reduce_fusion.2
  570.8 32.5 %reduce-scatter.15.cloned.1.call-done = bf16[512,1152]{1,0:T(8,128)(2,1)} async-done(((bf16[1024,1152]{1,0:T(8,128)(2,1)}), bf16[512,1152]{1,0:T(8,128)(2,1)}) %reduce-scatter.15.cloned.1.call-update) | async-done | bytes 1179664 | tf_op jit(solution)/shard_map/reduce_scatter | solution.py:166
  603.3 6.2 multiply_reduce_fusion.3
  612.1 36.2 %all-gather.27.cloned.1.call-done = bf16[1024,1152]{1,0:T(8,128)(2,1)} async-done(((bf16[512,1152]{1,0:T(8,128)(2,1)}), bf16[1024,1152]{1,0:T(8,128)(2,1)}) %all-gather.27.cloned.1.call-update) | async-done | bytes 2359312 | tf_op jit(solution)/shard_map/all_gather | solution.py:193
  648.2 4.8 convolution_convert_fusion.1
  653.1 4.0 reshape.171
  657.1 2.5 copy.48
  660.7 116.9 %while.28 = (s32[]{:T(128)}, f32[8,1024,72]{1,2,0:T(8,128)}, f32[8,1024,72]{1,2,0:T(8,128)}, bf16[2,8,512,72]{2,3,1,0:T(8,128)(2,1)}, bf16[2,8,512,72]{2,3,1,0:T...) while((s32[]{:T(128)}, f32[8,1024,72]{1,2,0:T(8,128)}, ...), condition=%wide.region_16.17_spmd.clone, body=%wide.region_14.16_spmd.clone.sunk | while | flops 3073470464 | bytes 271434112 | solution.py:238
  661.6 8.1 fusion.143
  669.8 10.3 select_add_fusion.5
  680.1 14.5 multiply_reduce_fusion.10
  697.0 10.5 multiply_convert_fusion.8
  707.5 7.3 fusion.144
  714.8 3.1 select_add_fusion.4
  718.7 8.1 fusion.143
  726.9 11.1 select_add_fusion.5
  738.0 14.5 multiply_reduce_fusion.10
  754.8 10.5 multiply_convert_fusion.8
  765.3 7.3 fusion.144
  772.7 4.9 select_add_fusion.4
  782.1 7.2 bitcast_convert_fusion
  789.3 5.7 fusion.84
  795.8 12.4 fusion.73
  808.3 11.5 fusion.85
  820.1 9.5 fusion.42
  834.6 2.9 fusion.61
  838.8 8.4 all-reduce.12
  847.2 7.3 broadcast_multiply_fusion
  859.3 4.9 convolution_reduce_fusion.1
  864.9 61.7 %all-reduce.10 = (f32[6912]{0:T(1024)}, f32[2,1152]{1,0:T(2,128)}, f32[1152]{0:T(1024)}, f32[4608]{0:T(1024)}, f32[1152]{0:T(1024)}) all-reduce(bf16[6912]{0:T(1024)(128)(2,1)} %copy-done.25, bf16[2,1152]{1,0:T(2,128)(2,1)} %get-tuple-element.224, f32[1152]{0:T(1024)} %convert_reduce_fusion.2, ...), channel_id=7, replica_groups=mesh['fsdp'=16,'tp'=2] {'fsdp'}, use_global_device_ids=true, to_apply=%region_28.29.clone | all-reduce | flops 16128 | bytes 101376
  934.5 3.2 fusion.69
  937.6 80.0 %reduce-scatter.27.cloned.1.call-done = f32[2304,72]{0,1:T(8,128)} async-done(((f32[2304,1152]{0,1:T(8,128)}), f32[2304,72]{0,1:T(8,128)}) %reduce-scatter.27.cloned.1.call-update) | async-done | bytes 663568 | tf_op jit(solution)/shard_map/reduce_scatter | solution.py:301
  1017.6 124.5 %reduce-scatter.25.cloned.1.call-done = f32[72,2304]{1,0:T(8,128)} async-done(((f32[1152,2304]{1,0:T(8,128)}), f32[72,2304]{1,0:T(8,128)}) %reduce-scatter.25.cloned.1.call-update) | async-done | bytes 663568 | tf_op jit(solution)/shard_map/reduce_scatter | solution.py:299
  1142.1 111.3 %reduce-scatter.23.cloned.1.call-done = f32[72,3,576]{2,0,1:T(8,128)} async-done(((f32[1152,3,576]{2,0,1:T(8,128)}), f32[72,3,576]{2,0,1:T(8,128)}) %reduce-scatter.23.cloned.1.call-update) | async-done | bytes 497680 | tf_op jit(solution)/shard_map/reduce_scatter | solution.py:295
  1253.5 191.4 %reduce-scatter.21.cloned.1.call-done = f32[576,432]{0,1:T(8,128)} async-done(((f32[576,6912]{0,1:T(8,128)}), f32[576,432]{0,1:T(8,128)}) %reduce-scatter.21.cloned.1.call-update) | async-done | bytes 995344 | tf_op jit(solution)/shard_map/reduce_scatter | solution.py:293
  (240 shorter events, 71.1 us)
Async XLA Ops:
  7.2 77.3 %copy-start.10 = (bf16[1,512,1152]{2,1,0:T(8,128)(2,1)S(1)}, bf16[1,512,1152]{2,1,0:T(8,128)(2,1)}, u32[]{:S(2)}) copy-start(bf16[1,512,1152]{2,1,0:T(8,128)(2,1)} %param.17) | copy-start | bytes 3538948
  7.2 84.4 %all-gather.11.cloned.1.call-start = ((), (), s32[]{:S(2)}) async-start(), calls=%async_computation.9 | async-start | bytes 9400320 | tf_op jit(solution)/shard_map/all_gather | solution.py:85
  7.9 135.8 %all-gather.15.cloned.1.call-start = ((), (), s32[]{:S(2)}) async-start(), calls=%async_computation.11 | async-start | bytes 4700160 | tf_op jit(solution)/shard_map/all_gather | solution.py:87
  8.7 171.8 %all-gather.13.cloned.1.call-start = ((), (), s32[]{:S(2)}) async-start(), calls=%async_computation.10 | async-start | bytes 3538944 | tf_op jit(solution)/shard_map/all_gather | solution.py:114
  84.5 21.9 %copy-start.29 = (f32[512]{0:T(512)}, f32[512]{0:T(512)S(1)}, u32[]{:S(2)}) copy-start(f32[512]{0:T(512)S(1)} %broadcast_multiply_fusion.6) | copy-start | bytes 6148
  85.0 21.5 %copy-start.34 = (f32[512]{0:T(512)}, f32[512]{0:T(512)S(1)}, u32[]{:S(2)}) copy-start(f32[512]{0:T(512)S(1)} %add_rsqrt_fusion.1) | copy-start | bytes 6148
  97.5 11.7 copy-start.45
  108.6 113.2 %all-gather.17.cloned.1.call-start = ((), (), s32[]{:S(2)}) async-start(), calls=%async_computation.12 | async-start | bytes 1566720 | tf_op jit(solution)/shard_map/all_gather | solution.py:89
  109.2 177.9 %reduce-scatter.13.cloned.1.call-start = ((), (), s32[]{:S(2)}) async-start(), calls=%async_computation.13 | async-start | bytes 7077888 | tf_op jit(solution)/shard_map/reduce_scatter | solution.py:148
  196.6 3.6 copy-start.16
  200.1 4.4 copy-start.20
  208.7 3.6 copy-start.16
  212.2 4.4 copy-start.20
  227.9 59.2 %copy-start.27 = (f32[1152]{0:T(1024)S(1)}, f32[1152]{0:T(1024)}, u32[]{:S(2)}) copy-start(f32[1152]{0:T(1024)} %get-tuple-element.247) | copy-start | bytes 13828
  227.9 117.8 %all-gather.21.cloned.1.call-start = ((), (), s32[]{:S(2)}) async-start(), calls=%async_computation.15 | async-start | bytes 5640192 | tf_op jit(solution)/shard_map/all_gather | solution.py:91
  228.5 154.1 %all-gather.19.cloned.1.call-start = ((), (), s32[]{:S(2)}) async-start(), calls=%async_computation.14 | async-start | bytes 3538944 | tf_op jit(solution)/shard_map/all_gather | solution.py:156
  229.3 57.8 %copy-start.28 = (f32[1152]{0:T(1024)}, f32[1152]{0:T(1024)S(1)}, u32[]{:S(2)}) copy-start(f32[1152]{0:T(1024)S(1)} %convert_element_type.164) | copy-start | bytes 13828
  292.5 148.9 %all-gather.23.cloned.1.call-start = ((), (), s32[]{:S(2)}) async-start(), calls=%async_computation.16 | async-start | bytes 5640192 | tf_op jit(solution)/shard_map/all_gather | solution.py:93
  293.2 185.0 %all-gather.25.cloned.1.call-start = ((), (), s32[]{:S(2)}) async-start(), calls=%async_computation.18 | async-start | bytes 3538944 | tf_op jit(solution)/shard_map/all_gather | solution.py:175
  295.8 270.5 %reduce-scatter.17.cloned.1.call-start = ((), (), s32[]{:S(2)}) async-start(), calls=%async_computation.19 | async-start | bytes 7077888 | tf_op jit(solution)/shard_map/reduce_scatter | solution.py:184
  493.6 2.1 copy-start.46
  506.1 97.2 %reduce-scatter.15.cloned.1.call-start = ((), (), s32[]{:S(2)}) async-start(), calls=%async_computation.17 | async-start | bytes 3538944 | tf_op jit(solution)/shard_map/reduce_scatter | solution.py:166
  520.1 128.1 %all-gather.27.cloned.1.call-start = ((), (), s32[]{:S(2)}) async-start(), calls=%async_computation.20 | async-start | bytes 3538944 | tf_op jit(solution)/shard_map/all_gather | solution.py:193
  612.0 220.7 %reduce-scatter.19.cloned.1.call-start = ((), (), s32[]{:S(2)}) async-start(), calls=%async_computation.21 | async-start | bytes 3538944 | tf_op jit(solution)/shard_map/reduce_scatter | solution.py:249
  660.8 8.9 copy-start.2
  660.9 8.9 copy-start.4
  660.9 8.9 copy-start.8
  680.1 16.9 %copy-start = (f32[8,512,1024]{2,1,0:T(8,128)S(1)}, f32[8,512,1024]{2,1,0:T(8,128)}, u32[]{:S(2)}) copy-start(f32[8,512,1024]{2,1,0:T(8,128)} %fusion.143) | copy-start | bytes 50331652 | tf_op jit(solution)/shard_map/while
  707.5 7.3 copy-start.1
  707.5 7.3 copy-start.5
  714.8 3.1 copy-start.3
  714.8 3.1 copy-start.9
  717.9 8.9 copy-start.2
  717.9 8.9 copy-start.4
  717.9 8.9 copy-start.8
  738.0 16.9 %copy-start = (f32[8,512,1024]{2,1,0:T(8,128)S(1)}, f32[8,512,1024]{2,1,0:T(8,128)}, u32[]{:S(2)}) copy-start(f32[8,512,1024]{2,1,0:T(8,128)} %fusion.143) | copy-start | bytes 50331652 | tf_op jit(solution)/shard_map/while
  765.3 7.3 copy-start.1
  765.3 7.3 copy-start.5
  772.6 5.0 copy-start.3
  772.6 5.0 copy-start.9
  777.6 2.0 copy-start.6
  777.6 4.5 slice-start
  779.6 2.4 slice-start.1
  782.1 38.0 %copy-start.14 = (bf16[1024,3,576]{0,2,1:T(8,128)(2,1)}, bf16[1024,3,576]{0,2,1:T(8,128)(2,1)S(1)}, u32[]{:S(2)}) copy-start(bf16[1024,3,576]{0,2,1:T(8,128)(2,1)S(1)} %maximum_convert_fusion) | copy-start | bytes 10616836
  789.3 148.3 %reduce-scatter.29.cloned.1.call-start = ((), (), s32[]{:S(2)}) async-start(), calls=%async_computation.26 | async-start | bytes 3133440
  795.1 222.5 %reduce-scatter.27.cloned.1.call-start = ((), (), s32[]{:S(2)}) async-start(), calls=%async_computation.25 | async-start | bytes 11280384 | tf_op jit(solution)/shard_map/reduce_scatter | solution.py:301
  808.2 333.9 %reduce-scatter.25.cloned.1.call-start = ((), (), s32[]{:S(2)}) async-start(), calls=%async_computation.24 | async-start | bytes 11280384 | tf_op jit(solution)/shard_map/reduce_scatter | solution.py:299
  819.8 433.7 %reduce-scatter.23.cloned.1.call-start = ((), (), s32[]{:S(2)}) async-start(), calls=%async_computation.23 | async-start | bytes 9400320 | tf_op jit(solution)/shard_map/reduce_scatter | solution.py:295
  829.6 5.0 copy-start.11
  829.6 5.0 copy-start.23
  829.6 5.0 copy-start.30
  829.6 5.0 copy-start.35
  829.6 615.2 %reduce-scatter.21.cloned.1.call-start = ((), (), s32[]{:S(2)}) async-start(), calls=%async_computation.22 | async-start | bytes 18800640 | tf_op jit(solution)/shard_map/reduce_scatter | solution.py:293
  832.5 5.3 copy-start.39
  832.5 5.5 copy-start.41
  832.5 5.8 copy-start.40
  832.5 6.1 copy-start.38
  832.5 14.7 %copy-start.42 = (f32[576]{0:T(1024)S(1)}, f32[576]{0:T(1024)}, u32[]{:S(2)}) copy-start(f32[576]{0:T(1024)} %get-tuple-element.226) | copy-start | bytes 6916
  847.2 7.3 copy-start.25
  854.5 2.1 copy-start.18
  856.6 1.7 copy-start.19
  856.6 2.7 copy-start.26
  859.3 5.0 copy-start.33
  859.3 75.1 %copy-start.13 = (f32[512,1152]{1,0:T(8,128)S(1)}, f32[512,1152]{1,0:T(8,128)}, u32[]{:S(2)}) copy-start(f32[512,1152]{1,0:T(8,128)} %copy-done.12) | copy-start | bytes 7077892
  (15 other events, 15.5 us)
Sparse Core Ops, SparseCore 0:
  10.2 81.3 all-gather.10
  93.8 49.8 all-gather.14
  145.8 34.5 all-gather.12
  182.4 39.3 all-gather.16
  228.1 58.9 reduce-scatter.12
  289.3 56.3 all-gather.20
  347.9 34.6 all-gather.18
  385.0 56.3 all-gather.22
  443.6 34.6 all-gather.24
  506.2 59.9 reduce-scatter.16
  568.5 34.7 reduce-scatter.14
  612.1 36.0 all-gather.26
  789.4 34.6 reduce-scatter.18
  828.5 65.4 reduce-scatter.28
  898.5 119.1 reduce-scatter.26
  1022.1 119.9 reduce-scatter.24
  1146.7 106.7 reduce-scatter.22
  1258.7 186.1 reduce-scatter.20
where the time goes:
time: 1460 us; the launch traced here: 1450 us
  waiting for transfers between devices  904 us (62%)
  matrix products  229 us (16%)
  blocking collectives  163 us (11%)
  other arithmetic  78.6 us (5%)
  local copies, waits for them, and re-layouts  56 us (4%)
  between operations  19.3 us (1%)
    reduce_scatter x1, waiting for transfers between devices, shards(): lax.psum_scatter(mod_weight_term, 'fsdp', scatter_dimension=1, tiled=True)  191 us
    unnamed x2, blocking collectives  127 us
    reduce_scatter x1, waiting for transfers between devices, shards(): lax.psum_scatter(up_weight_term, 'fsdp', scatter_dimension=0, tiled=True)  124 us
    reduce_scatter x1, waiting for transfers between devices, shards(): lax.psum_scatter(qkv_weight_term, 'fsdp', scatter_dimension=0, tiled=True)  111 us
    reduce_scatter x1, waiting for transfers between devices, shards(): lax.psum_scatter(down_weight_term, 'fsdp', scatter_dimension=1, tiled=True)  80 us
    reduce_scatter x1, waiting for transfers between devices, shards(): lax.psum_scatter(jnp.dot(picked, out_full, preferred_element_type=jnp.flo...  57.8 us
    all_gather x1, waiting for transfers between devices, shards(): lax.all_gather(up_weight, 'fsdp', axis=0, tiled=True)  48.3 us
    all_gather x1, waiting for transfers between devices, shards(): lax.all_gather(down_weight, 'fsdp', axis=1, tiled=True)  47.4 us
  transfers between devices with their start and end apart: 18, of which 16 were waited for; matrix products, arithmetic and copies ran while one was open for 12% of the time, Pallas kernels for 0%

commit v1 on v0

v1 whole, which is shorter than its diff:
```python
import math

import jax
import jax.numpy as jnp
from jax import lax
from jax.sharding import PartitionSpec as P

HEAD_DIM = 72


EPSILON = 1e-06
HIGH = lax.Precision.HIGHEST


def normalize(values):
    center = values - jnp.mean(values, axis=-1, keepdims=True)
    variance = jnp.mean(center * center, axis=-1, keepdims=True)
    inverse = lax.rsqrt(variance + EPSILON)
    return (center * inverse, inverse)


def norm_back(grad_norm, normed, inverse):
    first_mean = jnp.mean(grad_norm, axis=-1, keepdims=True)
    second_mean = jnp.mean(grad_norm * normed, axis=-1, keepdims=True)
    return inverse * (grad_norm - first_mean - normed * second_mean)


def inner_rows(left, right):
    return lax.dot_general(
        left, right, (((0,), (0,)), ((), ())), preferred_element_type=jnp.float32
    )


def outer_cols(left, right):
    return lax.dot_general(
        left, right, (((1,), (1,)), ((), ())), preferred_element_type=jnp.float32
    )


def gelu_tanh(values):
    return jax.nn.gelu(values, approximate=True)


def to_heads(flat, head_count):
    return flat.reshape(flat.shape[0], head_count, HEAD_DIM).transpose(1, 0, 2)


def from_heads(stacked):
    return stacked.transpose(1, 0, 2).reshape(stacked.shape[1], stacked.shape[0] * HEAD_DIM)


def swap(values):
    return lax.ppermute(values, "tp", [(0, 1), (1, 0)])


def gather_rows(values, tp_count):
    if tp_count == 2:
        return jnp.concatenate([values, swap(values)], axis=0)
    return lax.all_gather(values, "tp", axis=0, tiled=True)


def scatter_rows(left, right, contract, tp_count):
    if tp_count == 2:
        half = left.shape[0] // 2
        sent = swap(contract(left[half:], right).astype(jnp.bfloat16))
        return contract(left[:half], right) + sent.astype(jnp.float32)
    return lax.psum_scatter(
        contract(left, right).astype(jnp.bfloat16), "tp", scatter_dimension=0, tiled=True
    ).astype(jnp.float32)


def sum_pair(values, tp_count):
    if tp_count == 2:
        return values + swap(values)
    return lax.psum(values, "tp")


def plain(left, right):
    return jnp.dot(left, right, preferred_element_type=jnp.float32)


def reduce_grad(term, axis):
    return lax.psum_scatter(
        term.astype(jnp.bfloat16), "fsdp", scatter_dimension=axis, tiled=True
    )


def gather_small(flat):
    size = flat.shape[0]
    padded = -(-size // 1024) * 1024
    block = jnp.pad(flat, (0, padded - size)).reshape(8, padded // 8)
    return lax.all_gather(block, "fsdp", axis=0, tiled=True).reshape(-1, padded)[:, :size]


def trade(rows):
    return lax.all_to_all(rows, "fsdp", split_axis=0, concat_axis=0, tiled=True)


def shards(
    tokens,
    condition,
    mod_weight,
    mod_bias,
    qkv_weight,
    qv_bias,
    out_weight,
    out_bias,
    up_weight,
    up_bias,
    down_weight,
    down_bias,
    cotangent,
):
    tp_count = lax.axis_size("tp")
    tp_place = lax.axis_index("tp")
    fsdp_count = lax.axis_size("fsdp")
    local_rows = tokens.shape[1]
    width = tokens.shape[2]
    seq_len = local_rows * tp_count
    share = width // tp_count
    thin = width // fsdp_count
    hidden_thin = up_bias.shape[0]
    hidden_full = hidden_thin * fsdp_count
    mod_thin = mod_bias.shape[0]
    small = gather_small(
        jnp.concatenate([condition[0], qv_bias.reshape(-1), out_bias, up_bias, down_bias])
    ).astype(jnp.float32)
    qkv_full = lax.all_gather(qkv_weight, "fsdp", axis=0, tiled=True)
    out_full = lax.all_gather(out_weight, "fsdp", axis=1, tiled=True)
    up_full = lax.all_gather(up_weight, "fsdp", axis=0, tiled=True)
    down_full = lax.all_gather(down_weight, "fsdp", axis=1, tiled=True)
    cond_all = small[:, :width]
    spot = width
    qv_full = (
        small[:, spot : spot + 2 * thin]
        .reshape(fsdp_count, 2, thin)
        .transpose(1, 0, 2)
        .reshape(2, width)
    )
    spot += 2 * thin
    out_shift = small[:, spot : spot + thin].reshape(-1)
    spot += thin
    up_shift = small[:, spot : spot + hidden_thin].reshape(-1)
    spot += hidden_thin
    down_shift = small[:, spot : spot + thin].reshape(-1)
    head_cols = qkv_full.shape[2]
    head_count = head_cols // HEAD_DIM
    hidden_cols = up_full.shape[1]
    cond_part = lax.dynamic_slice_in_dim(cond_all, tp_place * share, share, 1)
    silu_low = jax.nn.silu(cond_part).astype(jnp.bfloat16)
    partial_mod = jnp.dot(silu_low, mod_weight, preferred_element_type=jnp.float32)
    modulation = trade(sum_pair(partial_mod, tp_count) + mod_bias.astype(jnp.float32)).reshape(-1)
    pieces = modulation.reshape(6, width)
    shift_one = pieces[0]
    scale_one = pieces[1]
    gate_one = pieces[2]
    shift_two = pieces[3]
    scale_two = pieces[4]
    gate_two = pieces[5]
    rows_in = tokens[0].astype(jnp.float32)
    normed_one, inverse_one = normalize(rows_in)
    hidden_one = gather_rows(
        (normed_one * (1.0 + scale_one) + shift_one).astype(jnp.bfloat16), tp_count
    )
    qkv_matrix = qkv_full.reshape(width, 3 * head_cols)
    projected = plain(hidden_one, qkv_matrix).reshape(seq_len, 3, head_cols)
    qv_local = lax.dynamic_slice_in_dim(qv_full, tp_place * head_cols, head_cols, 1)
    queries = to_heads((projected[:, 0] + qv_local[0]).astype(jnp.bfloat16), head_count)
    keys_all = to_heads(projected[:, 1].astype(jnp.bfloat16), head_count)
    values_all = to_heads((projected[:, 2] + qv_local[1]).astype(jnp.bfloat16), head_count)
    grad_rows = cotangent[0].astype(jnp.float32)
    grad_two_own = (grad_rows * gate_two).astype(jnp.bfloat16)
    grad_branch_two = gather_rows(grad_two_own, tp_count)
    block = min(512, seq_len)
    block_count = seq_len // block
    scaling = 1.0 / math.sqrt(HEAD_DIM)
    query_blocks = queries.reshape(head_count, block_count, block, HEAD_DIM).transpose(1, 0, 2, 3)

    def attend(query_block):
        scores = (
            jnp.einsum("hqd,hkd->hqk", query_block, keys_all, preferred_element_type=jnp.float32)
            * scaling
        )
        highest = jnp.max(scores, axis=-1, keepdims=True)
        raised = jnp.exp(scores - highest)
        totals = jnp.sum(raised, axis=-1, keepdims=True)
        weights = (raised / totals).astype(jnp.bfloat16)
        output = jnp.einsum("hqk,hkd->hqd", weights, values_all, preferred_element_type=jnp.float32)
        return (output, (highest + jnp.log(totals))[..., 0])

    attended_blocks, log_totals = lax.map(attend, query_blocks)
    attended = attended_blocks.transpose(1, 0, 2, 3).reshape(head_count, seq_len, HEAD_DIM)
    attended_low = from_heads(attended).astype(jnp.bfloat16)
    branch_one = scatter_rows(attended_low, out_full, plain, tp_count) + out_shift
    middle = rows_in + gate_one * branch_one
    normed_two, inverse_two = normalize(middle)
    hidden_two = gather_rows(
        (normed_two * (1.0 + scale_two) + shift_two).astype(jnp.bfloat16), tp_count
    )
    up_local = lax.dynamic_slice_in_dim(up_shift, tp_place * hidden_cols, hidden_cols)
    before = plain(hidden_two, up_full) + up_local
    activated, gelu_pull = jax.vjp(gelu_tanh, before)
    activated_low = activated.astype(jnp.bfloat16)
    grad_before = gelu_pull(outer_cols(grad_branch_two, down_full))[0].astype(jnp.bfloat16)
    grad_hidden_two = scatter_rows(grad_before, up_full, outer_cols, tp_count)
    branch_two = scatter_rows(activated_low, down_full, plain, tp_count) + down_shift
    outcome = (middle + gate_two * branch_two).astype(jnp.bfloat16)
    grad_gate_two = jnp.sum(grad_rows * branch_two, axis=0)
    down_bias_part = jnp.sum(grad_two_own.astype(jnp.float32), axis=0)
    down_grad = reduce_grad(inner_rows(activated_low, grad_branch_two), 1)
    up_bias_part = jnp.sum(grad_before.astype(jnp.float32), axis=0)
    up_grad = reduce_grad(inner_rows(hidden_two, grad_before), 0)
    grad_scale_two = jnp.sum(grad_hidden_two * normed_two, axis=0)
    grad_shift_two = jnp.sum(grad_hidden_two, axis=0)
    grad_middle = grad_rows + norm_back(
        grad_hidden_two * (1.0 + scale_two), normed_two, inverse_two
    )
    grad_gate_one = jnp.sum(grad_middle * branch_one, axis=0)
    grad_one_own = (grad_middle * gate_one).astype(jnp.bfloat16)
    grad_branch_one = gather_rows(grad_one_own, tp_count)
    out_bias_part = jnp.sum(grad_one_own.astype(jnp.float32), axis=0)
    out_grad = reduce_grad(inner_rows(attended_low, grad_branch_one), 1)
    grad_attended = outer_cols(grad_branch_one, out_full).astype(jnp.bfloat16)
    grad_blocks = (
        to_heads(grad_attended, head_count)
        .reshape(head_count, block_count, block, HEAD_DIM)
        .transpose(1, 0, 2, 3)
    )

    def attend_back(carry, inputs):
        grad_keys, grad_values = carry
        query_block, log_block, grad_block = inputs
        scores = (
            jnp.einsum("hqd,hkd->hqk", query_block, keys_all, preferred_element_type=jnp.float32)
            * scaling
        )
        weights = jnp.exp(scores - log_block[..., None])
        grad_weights = jnp.einsum(
            "hqd,hkd->hqk", grad_block, values_all, preferred_element_type=jnp.float32
        )
        centered = jnp.sum(weights * grad_weights, axis=-1, keepdims=True)
        grad_scores = (weights * (grad_weights - centered)).astype(jnp.bfloat16)
        grad_query = (
            jnp.einsum("hqk,hkd->hqd", grad_scores, keys_all, preferred_element_type=jnp.float32)
            * scaling
        )
        grad_keys = (
            grad_keys
            + jnp.einsum(
                "hqk,hqd->hkd", grad_scores, query_block, preferred_element_type=jnp.float32
            )
            * scaling
        )
        grad_values = grad_values + jnp.einsum(
            "hqk,hqd->hkd",
            weights.astype(jnp.bfloat16),
            grad_block,
            preferred_element_type=jnp.float32,
        )
        return ((grad_keys, grad_values), grad_query)

    zero_heads = jnp.zeros((head_count, seq_len, HEAD_DIM), jnp.float32)
    (grad_keys, grad_values), grad_query_blocks = lax.scan(
        attend_back, (zero_heads, zero_heads), (query_blocks, log_totals, grad_blocks)
    )
    grad_queries = grad_query_blocks.transpose(1, 0, 2, 3).reshape(head_count, seq_len, HEAD_DIM)
    grad_projected = jnp.stack(
        [from_heads(grad_queries), from_heads(grad_keys), from_heads(grad_values)], axis=1
    ).astype(jnp.bfloat16)
    grad_projected, down_grad, up_grad, out_grad = lax.optimization_barrier(
        (grad_projected, down_grad, up_grad, out_grad)
    )
    qv_bias_part = jnp.sum(grad_projected[:, 0::2].astype(jnp.float32), axis=0)
    grad_flat = grad_projected.reshape(seq_len, 3 * head_cols)
    grad_hidden_one = scatter_rows(grad_flat, qkv_matrix, outer_cols, tp_count)
    qkv_grad = reduce_grad(inner_rows(hidden_one, grad_flat).reshape(width, 3, head_cols), 0)
    grad_scale_one = jnp.sum(grad_hidden_one * normed_one, axis=0)
    grad_shift_one = jnp.sum(grad_hidden_one, axis=0)
    grad_tokens = grad_middle + norm_back(
        grad_hidden_one * (1.0 + scale_one), normed_one, inverse_one
    )
    grad_mod_part = jnp.concatenate(
        [
            grad_shift_one,
            grad_scale_one,
            grad_gate_one,
            grad_shift_two,
            grad_scale_two,
            grad_gate_two,
        ]
    )
    qv_padded = lax.dynamic_update_slice_in_dim(
        jnp.zeros((2, width), jnp.float32), qv_bias_part, tp_place * head_cols, 1
    )
    up_padded = lax.dynamic_update_slice_in_dim(
        jnp.zeros((hidden_full,), jnp.float32), up_bias_part, tp_place * hidden_cols, 0
    )
    packed = jnp.concatenate(
        [
            grad_mod_part.reshape(fsdp_count, mod_thin),
            qv_padded.reshape(2, fsdp_count, thin)
            .transpose(1, 0, 2)
            .reshape(fsdp_count, 2 * thin),
            out_bias_part.reshape(fsdp_count, thin),
            up_padded.reshape(fsdp_count, hidden_thin),
            down_bias_part.reshape(fsdp_count, thin),
        ],
        axis=1,
    )
    traded = sum_pair(trade(packed), tp_count)
    totals = jnp.sum(traded, axis=0)
    grad_mod = traded[:, :mod_thin]
    mod_weight_grad = lax.dot_general(
        silu_low.astype(jnp.float32), grad_mod, (((0,), (0,)), ((), ())), precision=HIGH
    )
    silu_parts = lax.dot_general(
        grad_mod, mod_weight.astype(jnp.float32), (((1,), (1,)), ((), ())), precision=HIGH
    )
    grad_silu = jnp.sum(trade(silu_parts), axis=0)
    cond_row = condition[0].astype(jnp.float32)
    own_part = lax.dynamic_slice_in_dim(cond_row, tp_place * share, share)
    cond_grad = jax.vjp(jax.nn.silu, own_part)[1](grad_silu)[0][None, :]
    spot = mod_thin
    qv_bias_grad = totals[spot : spot + 2 * thin].reshape(2, thin)
    spot += 2 * thin
    out_bias_grad = totals[spot : spot + thin]
    spot += thin
    up_bias_grad = totals[spot : spot + hidden_thin]
    spot += hidden_thin
    down_bias_grad = totals[spot : spot + thin]
    return (
        outcome[None],
        grad_tokens.astype(jnp.bfloat16)[None],
        cond_grad,
        mod_weight_grad,
        totals[:mod_thin],
        qkv_grad.astype(jnp.float32),
        qv_bias_grad,
        out_grad.astype(jnp.float32),
        out_bias_grad,
        up_grad.astype(jnp.float32),
        up_bias_grad,
        down_grad.astype(jnp.float32),
        down_bias_grad,
    )


def solution(mesh):
    return jax.shard_map(
        shards,
        mesh=mesh,
        in_specs=(
            P("fsdp", "tp", None),
            P("fsdp", None),
            P("tp", "fsdp"),
            P("fsdp"),
            P("fsdp", None, "tp"),
            P(None, "fsdp"),
            P("tp", "fsdp"),
            P("fsdp"),
            P("fsdp", "tp"),
            P("fsdp"),
            P("tp", "fsdp"),
            P("fsdp"),
            P("fsdp", "tp", None),
        ),
        out_specs=(
            P("fsdp", "tp", None),
            P("fsdp", "tp", None),
            P("fsdp", "tp"),
            P("tp", "fsdp"),
            P("fsdp"),
            P("fsdp", None, "tp"),
            P(None, "fsdp"),
            P("tp", "fsdp"),
            P("fsdp"),
            P("fsdp", "tp"),
            P("fsdp"),
            P("tp", "fsdp"),
            P("fsdp"),
        ),
        check_vma=False,
    )
```

time: 1460 us -> 677 us (0.46)
  waiting for transfers between devices: 904 us -> 243 us
  blocking collectives: 163 us -> 34.1 us
  local copies, waits for them, and re-layouts: 56 us -> 82.7 us
  other arithmetic: 78.6 us -> 54.2 us
  starting transfers between devices: 1.7 us -> 20.5 us
    reduce_scatter x8 -> x2, waiting for transfers between devices: 642 us -> 65.5 us  [reduce_grad(): lax.psum_scatter(term.astype(jnp.bfloat16), 'fsdp', scatter_dimension=axi...]
    all_gather x9 -> x4, waiting for transfers between devices: 259 us -> 16.5 us  [the longest x1 9.64 us: shards(): qkv_full = lax.all_gather(qkv_weight, 'fsdp', axis=0, tiled=True)]
    ppermute x0 -> x10, waiting for transfers between devices: none -> 149 us  [swap(): return lax.ppermute(values, 'tp', [(0, 1), (1, 0)])]
    unnamed x2 -> x0, blocking collectives: 127 us -> none
    psum x2 -> x0, blocking collectives: 16.7 us -> none  [the longest x1 8.38 us: shards(): lax.psum(grad_mod_part.astype(jnp.bfloat16), 'tp').astype(jnp.float32)]
    unnamed x94 -> x110, local copies, waits for them, and re-layouts: 24.7 us -> 40.1 us
    dot_general x6 -> x9, matrix products: 49.1 us -> 40.1 us  [the longest x6 37.7 us: plain(): return jnp.dot(left, right, preferred_element_type=jnp.float32)]
    dot_general x4 -> x6, matrix products: 37.7 us -> 46.6 us  [outer_cols(): lax.dot_general(left, right, (((1,), (1,)), ((), ())), preferred_element_...]
  transfers between devices with their start and end apart: 18 -> 20, of which waited for: 16 -> 15; matrix products, arithmetic and copies ran while one was open for 12% -> 41% of each run, Pallas kernels for 0% -> 0%
where the time goes in v1:
time: 677 us; the launch traced here: 673 us
  waiting for transfers between devices  243 us (36%)
  matrix products  223 us (33%)
  local copies, waits for them, and re-layouts  82.7 us (12%)
  other arithmetic  54.2 us (8%)
  blocking collectives  34.1 us (5%)
  starting transfers between devices  20.5 us (3%)
  between operations  15.2 us (2%)
    ppermute x10, waiting for transfers between devices, swap(): return lax.ppermute(values, 'tp', [(0, 1), (1, 0)])  149 us
    reduce_scatter x2, waiting for transfers between devices, reduce_grad(): lax.psum_scatter(term.astype(jnp.bfloat16), 'fsdp', scatter_dimension=axi...  65.5 us
    dot_general x6, matrix products, outer_cols(): lax.dot_general(left, right, (((1,), (1,)), ((), ())), preferred_element_...  46.6 us
    unnamed x110, local copies, waits for them, and re-layouts  40.1 us
    dot_general x6, matrix products, plain(): return jnp.dot(left, right, preferred_element_type=jnp.float32)  37.7 us
    dot_general x4, matrix products, inner_rows(): lax.dot_general(left, right, (((0,), (0,)), ((), ())), preferred_element_...  32.5 us
    dot_general x2, matrix products, attend_back(): jnp.einsum('hqd,hkd->hqk', grad_block, values_all, preferred_element_type...  29.2 us
    all_gather x1, blocking collectives, gather_small(): lax.all_gather(block, 'fsdp', axis=0, tiled=True).reshape(-1, padded)  23.3 us
  transfers between devices with their start and end apart: 20, of which 15 were waited for; matrix products, arithmetic and copies ran while one was open for 41% of the time, Pallas kernels for 0%

profile of v1, /device:TPU:0, one launch (start us, length us, event | category | flops | bytes accessed | tf_op | source)
XLA Modules:
  0.0 673.0 jit_solution(11910449368759546914)
XLA Ops:
  13.0 23.3 %all_gather.15 = bf16[128,256]{1,0:T(8,128)(2,1)S(1)} all-gather(bf16[8,256]{1,0:T(8,128)(2,1)S(1)} %reshape.202), channel_id=1, replica_groups=mesh['fsdp'=16,'tp'=2] {'fsdp'}, dimensions={0}, use_global_device_ids=true | all-gather | bytes 69632 | tf_op jit(solution)/shard_map/all_gather | solution.py:92
  41.4 3.5 all-to-all-start
  44.9 7.1 %all-to-all-done = f32[16,1,432]{2,1,0:T(1,128)S(1)} async-done(((f32[16,1,432]{2,1,0:T(1,128)}), f32[16,1,432]{2,1,0:T(1,128)S(1)}, u32[]{:S(2)}, u32[]{:S(2)}) %all-to-all-start) | async-done | bytes 27680 | tf_op jit(solution)/shard_map/all_to_all | solution.py:96
  55.5 9.6 %all-gather.5.cloned.1.call-done = bf16[1152,3,576]{2,0,1:T(8,128)(2,1)} async-done(((bf16[72,3,576]{2,0,1:T(8,128)(2,1)}), bf16[1152,3,576]{2,0,1:T(8,128)(2,1)}) %all-gather.5.cloned.1.call-update) | async-done | bytes 3981328 | tf_op jit(solution)/shard_map/all_gather | solution.py:128
  65.2 7.0 %copy.44 = bf16[1152,3,576]{0,2,1:T(8,128)(2,1)} copy(bf16[1152,3,576]{2,0,1:T(8,128)(2,1)} %all-gather.5.cloned.1.call-done) | data formatting | bytes 7962624 | tf_op jit(solution)/shard_map/all_gather | solution.py:128
  72.2 8.6 %collective-permute-done.1 = bf16[512,1152]{1,0:T(8,128)(2,1)S(1)} collective-permute-done((bf16[512,1152]{1,0:T(8,128)(2,1)S(1)}, bf16[512,1152]{1,0:T(8,128)(2,1)S(1)}, u32[]{:S(2)}, u32[]{:S(2)}) %collective-permute-start.1) | collective-permute-done | bytes 1179680 | tf_op jit(solution)/shard_map/ppermute | solution.py:53
  81.8 6.6 fusion.40
  96.9 23.9 %while.27 = (s32[]{:T(128)}, bf16[2,8,512,72]{2,3,1,0:T(8,128)(2,1)}, f32[2,8,512]{2,1,0:T(8,128)S(1)}, bf16[2,8,512,72]{2,3,1,0:T(8,128)(2,1)S(1)}, bf16[8,1024...) while((s32[]{:T(128)}, bf16[2,8,512,72]{2,3,1,0:T(8,128)(2,1)}, ...), condition=%wide.region_5.6_spmd, body=%wide.region_2.5_spmd.sunk | while | flops 1245704192 | bytes 68747440 | solution.py:191
  96.9 2.5 multiply_reduce_fusion.10
  99.5 3.7 fusion.151
  103.2 4.7 fusion.152
  108.9 2.5 multiply_reduce_fusion.10
  111.4 3.7 fusion.151
  115.1 4.7 fusion.152
  124.2 3.8 convolution_convert_fusion.6
  131.7 23.0 %collective-permute-done.2 = bf16[512,1152]{1,0:T(8,128)(2,1)} collective-permute-done((bf16[512,1152]{1,0:T(8,128)(2,1)}, bf16[512,1152]{1,0:T(8,128)(2,1)}, u32[]{:S(2)}, u32[]{:S(2)}) %collective-permute-start.2) | collective-permute-done | bytes 1179680 | tf_op jit(solution)/shard_map/ppermute | solution.py:53
  154.7 4.9 fusion.103
  164.3 3.2 convert_reduce_fusion.3
  168.1 22.9 %collective-permute-done.3 = bf16[512,1152]{1,0:T(8,128)(2,1)} collective-permute-done((bf16[512,1152]{1,0:T(8,128)(2,1)}, bf16[512,1152]{1,0:T(8,128)(2,1)}, u32[]{:S(2)}, u32[]{:S(2)}) %collective-permute-start.3) | collective-permute-done | bytes 1179680 | tf_op jit(solution)/shard_map/ppermute | solution.py:53
  191.0 14.3 %multiply_convert_fusion.1 = (bf16[1024,2304]{1,0:T(8,128)(2,1)}, f32[1024,2304]{1,0:T(8,128)}) fusion(f32[2304]{0:T(1024)S(1)} %dynamic_slice.28, bf16[1152,2304]{1,0:T(8,128)(2,1)} %all-gather.9.cloned.1.call-done, bf16[512,1152]{1,0:T(8,128)(2,1)} %collective-permute-done.3, bf16[512,1152]{1,0:T(8,128)(2,1)} %add_convert_fusion.1), kind=kOutput, calls=%fused_computation.53 | convolution fusion | flops 5464129536 | bytes 21832704 | tf_op jit(solution)/shard_map/dot_general | solution.py:79
  205.3 7.5 %collective-permute-done.5 = bf16[512,1152]{1,0:T(8,128)(2,1)} collective-permute-done((bf16[512,1152]{1,0:T(8,128)(2,1)}, bf16[512,1152]{1,0:T(8,128)(2,1)}, u32[]{:S(2)}, u32[]{:S(2)}) %collective-permute-start.5) | collective-permute-done | bytes 1179680 | tf_op jit(solution)/shard_map/ppermute | solution.py:53
  212.8 6.8 %all-gather.11.cloned.1.call-done = bf16[2304,1152]{0,1:T(8,128)(2,1)} async-done(((bf16[2304,72]{0,1:T(8,128)(2,1)}), bf16[2304,1152]{0,1:T(8,128)(2,1)}) %all-gather.11.cloned.1.call-update) | async-done | bytes 5308432 | tf_op jit(solution)/shard_map/all_gather | solution.py:131
  219.6 17.0 %convert_reduce_fusion = (f32[2304]{0:T(1024)}, bf16[1024,2304]{1,0:T(8,128)(2,1)}) fusion(f32[1024,2304]{1,0:T(8,128)} %get-tuple-element.259, f32[2304]{0:T(1024)S(1)} %dynamic_slice.28, bf16[2304,1152]{0,1:T(8,128)(2,1)} %all-gather.11.cloned.1.call-done, bf16[512,1152]{1,0:T(8,128)(2,1)} %collective-permute-done.5, bf16[512,1152]{1,0:T(8,128)(2,1)} %get-tuple-element.232), kind=kOutput, calls=%fused_computation.52 | convolution fusion | flops 5494798336 | bytes 21841920 | tf_op jit(solution)/shard_map/dot_general | solution.py:35
  236.7 5.1 convolution_convert_fusion.4
  243.3 3.2 convolution_convert_fusion.5
  247.2 5.0 fusion.67
  252.1 18.5 %collective-permute-done.6 = bf16[512,1152]{1,0:T(8,128)(2,1)S(1)} collective-permute-done((bf16[512,1152]{1,0:T(8,128)(2,1)S(1)}, bf16[512,1152]{1,0:T(8,128)(2,1)S(1)}, u32[]{:S(2)}, u32[]{:S(2)}) %collective-permute-start.6) | collective-permute-done | bytes 1179680 | tf_op jit(solution)/shard_map/ppermute | solution.py:53
  270.6 6.0 multiply_reduce_fusion.2
  276.6 18.6 %collective-permute-done.4 = bf16[512,1152]{1,0:T(8,128)(2,1)S(1)} collective-permute-done((bf16[512,1152]{1,0:T(8,128)(2,1)S(1)}, bf16[512,1152]{1,0:T(8,128)(2,1)S(1)}, u32[]{:S(2)}, u32[]{:S(2)}) %collective-permute-start.4) | collective-permute-done | bytes 1179680 | tf_op jit(solution)/shard_map/ppermute | solution.py:53
  295.2 4.1 fusion.62
  300.8 25.9 %collective-permute-done.7 = bf16[512,1152]{1,0:T(8,128)(2,1)S(1)} collective-permute-done((bf16[512,1152]{1,0:T(8,128)(2,1)S(1)}, bf16[512,1152]{1,0:T(8,128)(2,1)S(1)}, u32[]{:S(2)}, u32[]{:S(2)}) %collective-permute-start.7) | collective-permute-done | bytes 1179680 | tf_op jit(solution)/shard_map/ppermute | solution.py:53
  327.7 3.3 convolution_convert_fusion.3
  331.1 10.9 %convolution_convert_fusion.1 = bf16[2304,1152]{0,1:T(8,128)(2,1)} fusion(bf16[1024,2304]{1,0:T(8,128)(2,1)} %get-tuple-element.258, bf16[512,1152]{1,0:T(8,128)(2,1)} %collective-permute-done.5, bf16[512,1152]{1,0:T(8,128)(2,1)} %get-tuple-element.232), kind=kOutput, calls=%fused_computation.44 | convolution fusion | flops 5443190784 | bytes 12386304 | tf_op jit(solution)/shard_map/dot_general | solution.py:29
  342.1 10.7 %convolution_convert_fusion = bf16[1152,2304]{1,0:T(8,128)(2,1)} fusion(bf16[1024,2304]{1,0:T(8,128)(2,1)} %get-tuple-element.263, bf16[512,1152]{1,0:T(8,128)(2,1)} %collective-permute-done.3, bf16[512,1152]{1,0:T(8,128)(2,1)} %add_convert_fusion.1), kind=kOutput, calls=%fused_computation.43 | convolution fusion | flops 5443190784 | bytes 12386304 | tf_op jit(solution)/shard_map/dot_general | solution.py:29
  352.8 4.8 convolution_convert_fusion.7
  357.6 4.0 reshape.210
  361.6 2.5 copy.49
  365.2 116.8 %while.28 = (s32[]{:T(128)}, f32[8,1024,72]{1,2,0:T(8,128)}, f32[8,1024,72]{1,2,0:T(8,128)}, bf16[2,8,512,72]{2,3,1,0:T(8,128)(2,1)}, bf16[2,8,512,72]{2,3,1,0:T...) while((s32[]{:T(128)}, f32[8,1024,72]{1,2,0:T(8,128)}, ...), condition=%wide.region_12.13_spmd.clone, body=%wide.region_10.12_spmd.clone.sunk | while | flops 3073470464 | bytes 261996880 | solution.py:263
  365.4 8.1 %fusion.162 = f32[8,512,1024]{2,1,0:T(8,128)} fusion(bf16[8,1024,72]{1,2,0:T(8,128)(2,1)S(1)} %get-tuple-element.414, bf16[2,8,512,72]{2,3,1,0:T(8,128)(2,1)S(1)} %get-tuple-element.413, s32[]{:T(128)S(6)} %copy.83), kind=kOutput, calls=%fused_computation.29.clone.1 | convolution fusion | flops 603979776 | bytes 18546692 | tf_op jit(solution)/shard_map/while/body/eval_jaxpr/hqd,hkd->hqk/dot_general | solution.py:234
  373.5 10.4 %select_add_fusion.5 = f32[8,1024,72]{1,2,0:T(8,128)} fusion(f32[8,1024,72]{1,2,0:T(8,128)} %get-tuple-element.400, f32[8,512,1024]{2,1,0:T(8,128)} %fusion.162, f32[8,512]{1,0:T(8,128)S(1)} %dynamic-slice_bitcast_fusion.2, pred[]{:T(512)S(6)} %compare.4, bf16[2,8,512,72]{2,3,1,0:T(8,128)(2,1)} %get-tuple-element.416, s32[]{:T(128)S(6)} %copy.83), kind=kOutput, calls=%fused_computation.20.clone.1 | convolution fusion | flops 617742336 | bytes 22102020 | tf_op jit(solution)/shard_map/while/body/eval_jaxpr/hqk,hqd->hkd/dot_general | solution.py:254
  383.9 14.6 %multiply_reduce_fusion.11 = (f32[8,512]{1,0:T(8,128)S(1)}, f32[8,512,1024]{2,1,0:T(8,128)}) fusion(f32[8,512,1024]{2,1,0:T(8,128)} %fusion.162, f32[8,512]{1,0:T(8,128)S(1)} %dynamic-slice_bitcast_fusion.2, bf16[8,1024,72]{1,2,0:T(8,128)(2,1)} %get-tuple-element.417, bf16[2,8,512,72]{2,3,1,0:T(8,128)(2,1)} %get-tuple-element.416, s32[]{:T(128)S(6)} %copy.83), kind=kOutput, calls=%fused_computation.14.clone.1 | convolution fusion | flops 620752896 | bytes 35356676 | tf_op jit(solution)/shard_map/while/body/eval_jaxpr/hqd,hkd->hqk/dot_general | solution.py:238
  398.5 2.7 copy-done.1
  401.3 11.3 %multiply_convert_fusion.8 = bf16[8,512,1024]{2,1,0:T(8,128)(2,1)} fusion(f32[8,512,1024]{2,1,0:T(8,128)} %get-tuple-element.364, f32[8,512,1024]{2,1,0:T(8,128)S(1)} %copy-done.1, f32[8,512]{1,0:T(8,128)S(1)} %get-tuple-element.365, f32[8,512]{1,0:T(8,128)S(1)} %dynamic-slice_bitcast_fusion.2), kind=kLoop, calls=%fused_computation.13.clone.1 | loop fusion | flops 20971520 | bytes 41975808 | tf_op jit(solution)/shard_map/while/body/eval_jaxpr/convert_element_type | solution.py:242
  412.5 7.3 %fusion.163 = bf16[2,8,512,72]{2,3,1,0:T(8,128)(2,1)} fusion(bf16[2,8,512,72]{2,3,1,0:T(8,128)(2,1)} %get-tuple-element.401, s32[]{:T(128)S(6)} %copy.83, bf16[8,512,1024]{2,1,0:T(8,128)(2,1)} %multiply_convert_fusion.8, bf16[8,1024,72]{1,2,0:T(8,128)(2,1)} %copy-done.3), kind=kOutput, calls=%fused_computation.24.clone.1 | convolution fusion | flops 604274688 | bytes 10747908 | tf_op jit(solution)/shard_map/while/body/eval_jaxpr/hqk,hkd->hqd/dot_general | solution.py:244
  419.9 3.1 select_add_fusion.4
  423.0 8.1 %fusion.162 = f32[8,512,1024]{2,1,0:T(8,128)} fusion(bf16[8,1024,72]{1,2,0:T(8,128)(2,1)S(1)} %get-tuple-element.414, bf16[2,8,512,72]{2,3,1,0:T(8,128)(2,1)S(1)} %get-tuple-element.413, s32[]{:T(128)S(6)} %copy.83), kind=kOutput, calls=%fused_computation.29.clone.1 | convolution fusion | flops 603979776 | bytes 18546692 | tf_op jit(solution)/shard_map/while/body/eval_jaxpr/hqd,hkd->hqk/dot_general | solution.py:234
  431.1 11.1 %select_add_fusion.5 = f32[8,1024,72]{1,2,0:T(8,128)} fusion(f32[8,1024,72]{1,2,0:T(8,128)} %get-tuple-element.400, f32[8,512,1024]{2,1,0:T(8,128)} %fusion.162, f32[8,512]{1,0:T(8,128)S(1)} %dynamic-slice_bitcast_fusion.2, pred[]{:T(512)S(6)} %compare.4, bf16[2,8,512,72]{2,3,1,0:T(8,128)(2,1)} %get-tuple-element.416, s32[]{:T(128)S(6)} %copy.83), kind=kOutput, calls=%fused_computation.20.clone.1 | convolution fusion | flops 617742336 | bytes 22102020 | tf_op jit(solution)/shard_map/while/body/eval_jaxpr/hqk,hqd->hkd/dot_general | solution.py:254
  442.2 14.6 %multiply_reduce_fusion.11 = (f32[8,512]{1,0:T(8,128)S(1)}, f32[8,512,1024]{2,1,0:T(8,128)}) fusion(f32[8,512,1024]{2,1,0:T(8,128)} %fusion.162, f32[8,512]{1,0:T(8,128)S(1)} %dynamic-slice_bitcast_fusion.2, bf16[8,1024,72]{1,2,0:T(8,128)(2,1)} %get-tuple-element.417, bf16[2,8,512,72]{2,3,1,0:T(8,128)(2,1)} %get-tuple-element.416, s32[]{:T(128)S(6)} %copy.83), kind=kOutput, calls=%fused_computation.14.clone.1 | convolution fusion | flops 620752896 | bytes 35356676 | tf_op jit(solution)/shard_map/while/body/eval_jaxpr/hqd,hkd->hqk/dot_general | solution.py:238
  456.8 2.4 copy-done.1
  459.3 10.5 %multiply_convert_fusion.8 = bf16[8,512,1024]{2,1,0:T(8,128)(2,1)} fusion(f32[8,512,1024]{2,1,0:T(8,128)} %get-tuple-element.364, f32[8,512,1024]{2,1,0:T(8,128)S(1)} %copy-done.1, f32[8,512]{1,0:T(8,128)S(1)} %get-tuple-element.365, f32[8,512]{1,0:T(8,128)S(1)} %dynamic-slice_bitcast_fusion.2), kind=kLoop, calls=%fused_computation.13.clone.1 | loop fusion | flops 20971520 | bytes 41975808 | tf_op jit(solution)/shard_map/while/body/eval_jaxpr/convert_element_type | solution.py:242
  469.8 7.3 %fusion.163 = bf16[2,8,512,72]{2,3,1,0:T(8,128)(2,1)} fusion(bf16[2,8,512,72]{2,3,1,0:T(8,128)(2,1)} %get-tuple-element.401, s32[]{:T(128)S(6)} %copy.83, bf16[8,512,1024]{2,1,0:T(8,128)(2,1)} %multiply_convert_fusion.8, bf16[8,1024,72]{1,2,0:T(8,128)(2,1)} %copy-done.3), kind=kOutput, calls=%fused_computation.24.clone.1 | convolution fusion | flops 604274688 | bytes 10747908 | tf_op jit(solution)/shard_map/while/body/eval_jaxpr/hqk,hkd->hqd/dot_general | solution.py:244
  477.1 4.9 select_add_fusion.4
  485.8 2.3 pad_maximum_fusion
  488.1 65.5 %reduce-scatter.11.cloned.1.call-done = bf16[72,2304]{1,0:T(8,128)(2,1)} async-done(((bf16[1152,2304]{1,0:T(8,128)(2,1)}), bf16[72,2304]{1,0:T(8,128)(2,1)}) %reduce-scatter.11.cloned.1.call-update) | async-done | bytes 331792 | tf_op jit(solution)/shard_map/reduce_scatter | solution.py:83
  553.6 7.6 %convolution_convert_fusion.2 = bf16[1152,3,576]{2,0,1:T(8,128)(2,1)S(1)} fusion(bf16[1024,3,576]{0,2,1:T(8,128)(2,1)} %pad_maximum_fusion, bf16[512,1152]{1,0:T(8,128)(2,1)S(1)} %copy-done.56, bf16[512,1152]{1,0:T(8,128)(2,1)S(1)} %copy-done.24), kind=kOutput, calls=%fused_computation.54 | convolution fusion | flops 4083572736 | bytes 9879552 | tf_op jit(solution)/shard_map/dot_general | solution.py:29
  561.3 18.2 %copy.56 = bf16[1152,3,576]{2,1,0:T(4,128)(2,1)} copy(bf16[1152,3,576]{2,0,1:T(8,128)(2,1)S(1)} %convolution_convert_fusion.2) | data formatting | bytes 7962624
  579.5 12.3 %reshape.225 = bf16[1152,1728]{1,0:T(8,128)(2,1)} reshape(bf16[1152,3,576]{2,1,0:T(4,128)(2,1)} %copy.56) | data formatting | bytes 7962624
  591.8 6.8 %fusion.43 = bf16[512,1152]{1,0:T(8,128)(2,1)} fusion(bf16[1152,3,576]{2,0,1:T(8,128)(2,1)} %all-gather.5.cloned.1.call-done, bf16[1024,3,576]{0,2,1:T(8,128)(2,1)} %pad_maximum_fusion), kind=kOutput, calls=%fused_computation.66 | convolution fusion | flops 2039021568 | bytes 7372800 | tf_op jit(solution)/shard_map/dot_general | solution.py:35
  603.7 21.9 %collective-permute-done.8 = bf16[512,1152]{1,0:T(8,128)(2,1)} collective-permute-done((bf16[512,1152]{1,0:T(8,128)(2,1)}, bf16[512,1152]{1,0:T(8,128)(2,1)}, u32[]{:S(2)}, u32[]{:S(2)}) %collective-permute-start.8) | collective-permute-done | bytes 1179680 | tf_op jit(solution)/shard_map/ppermute | solution.py:53
  625.6 6.9 %fusion.59 = (f32[1152]{0:T(1024)S(1)}, f32[512]{0:T(512)S(1)}, f32[512]{0:T(512)S(1)}, f32[1152]{0:T(1024)S(1)}, f32[512,1152]{1,0:T(8,128)S(1)}) fusion(bf16[1,512,1152]{2,1,0:T(8,128)(2,1)S(1)} %copy-done.13, f32[512]{0:T(512)S(1)} %copy-done.48, f32[512]{0:T(512)S(1)} %copy-done.44, f32[1152]{0:T(1024)S(1)} %copy-done.35, ...), kind=kOutput, calls=%fused_computation.87 | convolution fusion | flops 2045506304 | bytes 10933760 | tf_op jit(solution)/shard_map/dot_general | solution.py:35
  632.7 3.5 multiply_reduce_fusion.3
  636.6 10.7 %all_to_all.30 = f32[16,1,1008]{2,1,0:T(1,128)S(1)} all-to-all(f32[16,1,1008]{2,1,0:T(1,128)S(1)} %all_to_all.22), channel_id=1, replica_groups=mesh['fsdp'=16,'tp'=2] {'fsdp'}, dimensions={0} | all-to-all | bytes 129024 | tf_op jit(solution)/shard_map/all_to_all | solution.py:96
  652.7 3.5 all-to-all-start.2
  660.4 2.8 all-to-all-done.2
  (266 shorter events, 65.6 us)
Async XLA Ops:
  7.2 29.3 %copy-start = (bf16[576,432]{0,1:T(8,128)(2,1)S(1)}, bf16[576,432]{0,1:T(8,128)(2,1)}, u32[]{:S(2)}) copy-start(bf16[576,432]{0,1:T(8,128)(2,1)} %param.19) | copy-start | bytes 1492996
  7.2 31.1 %copy-start.12 = (bf16[1,512,1152]{2,1,0:T(8,128)(2,1)S(1)}, bf16[1,512,1152]{2,1,0:T(8,128)(2,1)}, u32[]{:S(2)}) copy-start(bf16[1,512,1152]{2,1,0:T(8,128)(2,1)} %param.17) | copy-start | bytes 3538948
  7.2 31.8 %copy-start.52 = (bf16[432]{0:T(512)(128)(2,1)S(1)}, bf16[432]{0:T(512)(128)(2,1)}, u32[]{:S(2)}) copy-start(bf16[432]{0:T(512)(128)(2,1)} %param.20) | copy-start | bytes 2596
  7.2 57.9 %all-gather.5.cloned.1.call-start = ((), (), s32[]{:S(2)}) async-start(), calls=%async_computation.7 | async-start | bytes 4700160 | tf_op jit(solution)/shard_map/all_gather | solution.py:128
  8.0 116.3 %all-gather.7.cloned.1.call-start = ((), (), s32[]{:S(2)}) async-start(), calls=%async_computation.8 | async-start | bytes 1566720 | tf_op jit(solution)/shard_map/all_gather | solution.py:129
  8.7 182.3 %all-gather.9.cloned.1.call-start = ((), (), s32[]{:S(2)}) async-start(), calls=%async_computation.9 | async-start | bytes 5640192 | tf_op jit(solution)/shard_map/all_gather | solution.py:130
  36.4 18.6 %copy-start.25 = (f32[16,1728]{1,0:T(8,128)}, f32[16,1728]{1,0:T(8,128)S(1)}, u32[]{:S(2)}) copy-start(f32[16,1728]{1,0:T(8,128)S(1)} %slice_convert_fusion.1) | copy-start | bytes 331780
  36.5 16.4 %copy-start.28 = (f32[16,1152]{1,0:T(8,128)}, f32[16,1152]{1,0:T(8,128)S(1)}, u32[]{:S(2)}) copy-start(f32[16,1152]{1,0:T(8,128)S(1)} %slice.148) | copy-start | bytes 221188
  36.8 3.9 collective-permute-start
  38.5 16.5 %copy-start.43 = (f32[512]{0:T(512)}, f32[512]{0:T(512)S(1)}, u32[]{:S(2)}) copy-start(f32[512]{0:T(512)S(1)} %broadcast_multiply_fusion.5) | copy-start | bytes 6148
  41.4 10.7 %all-to-all-start = ((f32[16,1,432]{2,1,0:T(1,128)}), f32[16,1,432]{2,1,0:T(1,128)S(1)}, u32[]{:S(2)}, u32[]{:S(2)}) async-start(f32[16,1,432]{2,1,0:T(1,128)} %copy.43), calls=%async_computation | async-start | bytes 65536 | tf_op jit(solution)/shard_map/all_to_all | solution.py:96
  44.9 174.8 %all-gather.11.cloned.1.call-start = ((), (), s32[]{:S(2)}) async-start(), calls=%async_computation.10 | async-start | bytes 5640192 | tf_op jit(solution)/shard_map/all_gather | solution.py:131
  44.9 10.1 %copy-start.47 = (f32[512]{0:T(512)}, f32[512]{0:T(512)S(1)}, u32[]{:S(2)}) copy-start(f32[512]{0:T(512)S(1)} %add_rsqrt_fusion.1) | copy-start | bytes 6148
  53.5 27.3 %copy-start.23 = (bf16[512,1152]{1,0:T(8,128)(2,1)}, bf16[512,1152]{1,0:T(8,128)(2,1)S(1)}, u32[]{:S(2)}) copy-start(bf16[512,1152]{1,0:T(8,128)(2,1)S(1)} %fusion.53) | copy-start | bytes 3538948
  53.5 27.3 %collective-permute-start.1 = (bf16[512,1152]{1,0:T(8,128)(2,1)S(1)}, bf16[512,1152]{1,0:T(8,128)(2,1)S(1)}, u32[]{:S(2)}, u32[]{:S(2)}) collective-permute-start(bf16[512,1152]{1,0:T(8,128)(2,1)S(1)} %fusion.53), channel_id=1, source_target_pairs={{0,1},{1,0},{2,3},{3,2},{4,5},{5,4},{6,7},{7,6},{8,9},{9,8},{10,11... | collective-permute-start | bytes 3538952 | tf_op jit(solution)/shard_map/ppermute | solution.py:53
  55.0 433.1 %reduce-scatter.15.cloned.1.call-start = ((), (), s32[]{:S(2)}) async-start(), calls=%async_computation.14 | async-start | bytes 1566720
  124.2 30.5 %copy-start.33 = (f32[1152]{0:T(1024)S(1)}, f32[1152]{0:T(1024)}, u32[]{:S(2)}) copy-start(f32[1152]{0:T(1024)} %get-tuple-element.196) | copy-start | bytes 13828
  128.0 26.7 %collective-permute-start.2 = (bf16[512,1152]{1,0:T(8,128)(2,1)}, bf16[512,1152]{1,0:T(8,128)(2,1)}, u32[]{:S(2)}, u32[]{:S(2)}) collective-permute-start(bf16[512,1152]{1,0:T(8,128)(2,1)} %convolution_convert_fusion.6), channel_id=1, source_target_pairs={{0,1},{1,0},{2,3},{3,2},{4,5},{5,4},{6,7},{7,6},{8,9},{9,8},{10,11... | collective-permute-start | bytes 3538952 | tf_op jit(solution)/shard_map/ppermute | solution.py:53
  131.7 27.9 %copy-start.36 = (f32[1152]{0:T(1024)}, f32[1152]{0:T(1024)S(1)}, u32[]{:S(2)}) copy-start(f32[1152]{0:T(1024)S(1)} %add.213) | copy-start | bytes 13828
  161.8 29.2 %collective-permute-start.3 = (bf16[512,1152]{1,0:T(8,128)(2,1)}, bf16[512,1152]{1,0:T(8,128)(2,1)}, u32[]{:S(2)}, u32[]{:S(2)}) collective-permute-start(bf16[512,1152]{1,0:T(8,128)(2,1)} %add_convert_fusion.1), channel_id=1, source_target_pairs={{0,1},{1,0},{2,3},{3,2},{4,5},{5,4},{6,7},{7,6},{8,9},{9,8},{10,11... | collective-permute-start | bytes 3538952 | tf_op jit(solution)/shard_map/ppermute | solution.py:53
  167.5 45.3 %collective-permute-start.5 = (bf16[512,1152]{1,0:T(8,128)(2,1)}, bf16[512,1152]{1,0:T(8,128)(2,1)}, u32[]{:S(2)}, u32[]{:S(2)}) collective-permute-start(bf16[512,1152]{1,0:T(8,128)(2,1)} %get-tuple-element.232), channel_id=1, source_target_pairs={{0,1},{1,0},{2,3},{3,2},{4,5},{5,4},{6,7},{7,6},{8,9},{9,8},{10,11... | collective-permute-start | bytes 3538952 | tf_op jit(solution)/shard_map/ppermute | solution.py:53
  219.6 17.0 %copy-start.53 = (bf16[1152,2304]{1,0:T(8,128)(2,1)S(1)}, bf16[1152,2304]{1,0:T(8,128)(2,1)}, u32[]{:S(2)}) copy-start(bf16[1152,2304]{1,0:T(8,128)(2,1)} %all-gather.9.cloned.1.call-done) | copy-start | bytes 15925252
  236.7 6.6 copy-start.54
  236.7 6.6 copy-start.58
  241.7 28.9 %collective-permute-start.6 = (bf16[512,1152]{1,0:T(8,128)(2,1)S(1)}, bf16[512,1152]{1,0:T(8,128)(2,1)S(1)}, u32[]{:S(2)}, u32[]{:S(2)}) collective-permute-start(bf16[512,1152]{1,0:T(8,128)(2,1)S(1)} %convolution_convert_fusion.4), channel_id=1, source_target_pairs={{0,1},{1,0},{2,3},{3,2},{4,5},{5,4},{6,7},{7,6},{8,9},{9,8},{10,11... | collective-permute-start | bytes 3538952 | tf_op jit(solution)/shard_map/ppermute | solution.py:53
  246.5 24.1 %copy-start.11 = (f32[512,1152]{1,0:T(8,128)S(1)}, f32[512,1152]{1,0:T(8,128)}, u32[]{:S(2)}) copy-start(f32[512,1152]{1,0:T(8,128)} %copy-done.10) | copy-start | bytes 7077892
  246.5 48.7 %collective-permute-start.4 = (bf16[512,1152]{1,0:T(8,128)(2,1)S(1)}, bf16[512,1152]{1,0:T(8,128)(2,1)S(1)}, u32[]{:S(2)}, u32[]{:S(2)}) collective-permute-start(bf16[512,1152]{1,0:T(8,128)(2,1)S(1)} %convolution_convert_fusion.5), channel_id=1, source_target_pairs={{0,1},{1,0},{2,3},{3,2},{4,5},{5,4},{6,7},{7,6},{8,9},{9,8},{10,11... | collective-permute-start | bytes 3538952 | tf_op jit(solution)/shard_map/ppermute | solution.py:53
  252.1 43.1 %copy-start.17 = (bf16[1,512,1152]{2,1,0:T(8,128)(2,1)S(1)}, bf16[1,512,1152]{2,1,0:T(8,128)(2,1)}, u32[]{:S(2)}) copy-start(bf16[1,512,1152]{2,1,0:T(8,128)(2,1)} %param.29) | copy-start | bytes 3538948
  295.2 32.5 %copy-start.19 = (bf16[2,8,9,8,512]{4,3,0,2,1:T(8,128)(2,1)S(1)}, bf16[2,8,9,8,512]{4,3,0,2,1:T(8,128)(2,1)}, u32[]{:S(2)}) copy-start(bf16[2,8,9,8,512]{4,3,0,2,1:T(8,128)(2,1)} %copy-done.18) | copy-start | bytes 3538948
  299.3 27.3 %copy-start.22 = (bf16[512,1152]{1,0:T(8,128)(2,1)}, bf16[512,1152]{1,0:T(8,128)(2,1)S(1)}, u32[]{:S(2)}) copy-start(bf16[512,1152]{1,0:T(8,128)(2,1)S(1)} %get-tuple-element.247) | copy-start | bytes 3538948
  299.3 27.3 %collective-permute-start.7 = (bf16[512,1152]{1,0:T(8,128)(2,1)S(1)}, bf16[512,1152]{1,0:T(8,128)(2,1)S(1)}, u32[]{:S(2)}, u32[]{:S(2)}) collective-permute-start(bf16[512,1152]{1,0:T(8,128)(2,1)S(1)} %get-tuple-element.247), channel_id=1, source_target_pairs={{0,1},{1,0},{2,3},{3,2},{4,5},{5,4},{6,7},{7,6},{8,9},{9,8},{10,11... | collective-permute-start | bytes 3538952 | tf_op jit(solution)/shard_map/ppermute | solution.py:53
  331.0 157.1 %reduce-scatter.9.cloned.1.call-start = ((), (), s32[]{:S(2)}) async-start(), calls=%async_computation.11 | async-start | bytes 5640192 | tf_op jit(solution)/shard_map/reduce_scatter | solution.py:83
  342.0 211.6 %reduce-scatter.11.cloned.1.call-start = ((), (), s32[]{:S(2)}) async-start(), calls=%async_computation.12 | async-start | bytes 5640192 | tf_op jit(solution)/shard_map/reduce_scatter | solution.py:83
  352.8 311.1 %reduce-scatter.13.cloned.1.call-start = ((), (), s32[]{:S(2)}) async-start(), calls=%async_computation.13 | async-start | bytes 4386816
  365.4 8.2 %copy-start.3 = (bf16[8,1024,72]{1,2,0:T(8,128)(2,1)}, bf16[8,1024,72]{1,2,0:T(8,128)(2,1)S(1)}, u32[]{:S(2)}) copy-start(bf16[8,1024,72]{1,2,0:T(8,128)(2,1)S(1)} %get-tuple-element.414) | copy-start | bytes 3538948 | tf_op jit(solution)/shard_map/while
  365.4 8.2 %copy-start.5 = (bf16[2,8,512,72]{2,3,1,0:T(8,128)(2,1)}, bf16[2,8,512,72]{2,3,1,0:T(8,128)(2,1)S(1)}, u32[]{:S(2)}) copy-start(bf16[2,8,512,72]{2,3,1,0:T(8,128)(2,1)S(1)} %get-tuple-element.413) | copy-start | bytes 3538948 | tf_op jit(solution)/shard_map/while
  383.9 17.4 %copy-start.1 = (f32[8,512,1024]{2,1,0:T(8,128)S(1)}, f32[8,512,1024]{2,1,0:T(8,128)}, u32[]{:S(2)}) copy-start(f32[8,512,1024]{2,1,0:T(8,128)} %fusion.162) | copy-start | bytes 50331652 | tf_op jit(solution)/shard_map/while
  412.5 7.3 %copy-start.2 = (bf16[8,512,1024]{2,1,0:T(8,128)(2,1)S(1)}, bf16[8,512,1024]{2,1,0:T(8,128)(2,1)}, u32[]{:S(2)}) copy-start(bf16[8,512,1024]{2,1,0:T(8,128)(2,1)} %multiply_convert_fusion.8) | copy-start | bytes 25165828 | tf_op jit(solution)/shard_map/while
  412.5 7.3 %copy-start.6 = (bf16[2,8,512,72]{2,3,1,0:T(8,128)(2,1)S(1)}, bf16[2,8,512,72]{2,3,1,0:T(8,128)(2,1)}, u32[]{:S(2)}) copy-start(bf16[2,8,512,72]{2,3,1,0:T(8,128)(2,1)} %copy-done.5) | copy-start | bytes 3538948 | tf_op jit(solution)/shard_map/while
  423.0 8.2 %copy-start.3 = (bf16[8,1024,72]{1,2,0:T(8,128)(2,1)}, bf16[8,1024,72]{1,2,0:T(8,128)(2,1)S(1)}, u32[]{:S(2)}) copy-start(bf16[8,1024,72]{1,2,0:T(8,128)(2,1)S(1)} %get-tuple-element.414) | copy-start | bytes 3538948 | tf_op jit(solution)/shard_map/while
  423.0 8.2 %copy-start.5 = (bf16[2,8,512,72]{2,3,1,0:T(8,128)(2,1)}, bf16[2,8,512,72]{2,3,1,0:T(8,128)(2,1)S(1)}, u32[]{:S(2)}) copy-start(bf16[2,8,512,72]{2,3,1,0:T(8,128)(2,1)S(1)} %get-tuple-element.413) | copy-start | bytes 3538948 | tf_op jit(solution)/shard_map/while
  442.2 17.0 %copy-start.1 = (f32[8,512,1024]{2,1,0:T(8,128)S(1)}, f32[8,512,1024]{2,1,0:T(8,128)}, u32[]{:S(2)}) copy-start(f32[8,512,1024]{2,1,0:T(8,128)} %fusion.162) | copy-start | bytes 50331652 | tf_op jit(solution)/shard_map/while
  469.7 7.3 %copy-start.2 = (bf16[8,512,1024]{2,1,0:T(8,128)(2,1)S(1)}, bf16[8,512,1024]{2,1,0:T(8,128)(2,1)}, u32[]{:S(2)}) copy-start(bf16[8,512,1024]{2,1,0:T(8,128)(2,1)} %multiply_convert_fusion.8) | copy-start | bytes 25165828 | tf_op jit(solution)/shard_map/while
  469.8 7.3 %copy-start.6 = (bf16[2,8,512,72]{2,3,1,0:T(8,128)(2,1)S(1)}, bf16[2,8,512,72]{2,3,1,0:T(8,128)(2,1)}, u32[]{:S(2)}) copy-start(bf16[2,8,512,72]{2,3,1,0:T(8,128)(2,1)} %copy-done.5) | copy-start | bytes 3538948 | tf_op jit(solution)/shard_map/while
  485.8 67.8 %copy-start.24 = (bf16[512,1152]{1,0:T(8,128)(2,1)S(1)}, bf16[512,1152]{1,0:T(8,128)(2,1)}, u32[]{:S(2)}) copy-start(bf16[512,1152]{1,0:T(8,128)(2,1)} %copy-done.23) | copy-start | bytes 3538948
  485.8 67.8 %copy-start.56 = (bf16[512,1152]{1,0:T(8,128)(2,1)S(1)}, bf16[512,1152]{1,0:T(8,128)(2,1)}, u32[]{:S(2)}) copy-start(bf16[512,1152]{1,0:T(8,128)(2,1)} %copy-done.55) | copy-start | bytes 3538948
  591.8 8.4 %copy-start.40 = (f32[1152]{0:T(1024)S(1)}, f32[1152]{0:T(1024)}, u32[]{:S(2)}) copy-start(f32[1152]{0:T(1024)} %get-tuple-element.231) | copy-start | bytes 13828
  591.8 8.5 %copy-start.49 = (f32[2304]{0:T(1024)S(1)}, f32[2304]{0:T(1024)}, u32[]{:S(2)}) copy-start(f32[2304]{0:T(1024)} %get-tuple-element.262) | copy-start | bytes 27652
  591.8 8.9 %copy-start.41 = (f32[1152]{0:T(1024)S(1)}, f32[1152]{0:T(1024)}, u32[]{:S(2)}) copy-start(f32[1152]{0:T(1024)} %get-tuple-element.246) | copy-start | bytes 13828
  598.6 27.0 %copy-start.13 = (bf16[1,512,1152]{2,1,0:T(8,128)(2,1)S(1)}, bf16[1,512,1152]{2,1,0:T(8,128)(2,1)}, u32[]{:S(2)}) copy-start(bf16[1,512,1152]{2,1,0:T(8,128)(2,1)} %param.17) | copy-start | bytes 3538948
  598.6 27.0 %copy-start.35 = (f32[1152]{0:T(1024)S(1)}, f32[1152]{0:T(1024)}, u32[]{:S(2)}) copy-start(f32[1152]{0:T(1024)} %copy-done.34) | copy-start | bytes 13828
  598.6 27.0 %copy-start.44 = (f32[512]{0:T(512)S(1)}, f32[512]{0:T(512)}, u32[]{:S(2)}) copy-start(f32[512]{0:T(512)} %copy-done.43) | copy-start | bytes 6148
  598.6 27.0 %copy-start.48 = (f32[512]{0:T(512)S(1)}, f32[512]{0:T(512)}, u32[]{:S(2)}) copy-start(f32[512]{0:T(512)} %copy-done.47) | copy-start | bytes 6148
  598.6 27.0 %collective-permute-start.8 = (bf16[512,1152]{1,0:T(8,128)(2,1)}, bf16[512,1152]{1,0:T(8,128)(2,1)}, u32[]{:S(2)}, u32[]{:S(2)}) collective-permute-start(bf16[512,1152]{1,0:T(8,128)(2,1)} %fusion.43), channel_id=1, source_target_pairs={{0,1},{1,0},{2,3},{3,2},{4,5},{5,4},{6,7},{7,6},{8,9},{9,8},{10,11... | collective-permute-start | bytes 3538952 | tf_op jit(solution)/shard_map/ppermute | solution.py:53
  603.7 28.9 %copy-start.14 = (f32[512,1152]{1,0:T(8,128)S(1)}, f32[512,1152]{1,0:T(8,128)}, u32[]{:S(2)}) copy-start(f32[512,1152]{1,0:T(8,128)} %get-tuple-element.257) | copy-start | bytes 7077892
  603.7 28.9 %copy-start.16 = (f32[512,1152]{1,0:T(8,128)S(1)}, f32[512,1152]{1,0:T(8,128)}, u32[]{:S(2)}) copy-start(f32[512,1152]{1,0:T(8,128)} %get-tuple-element.248) | copy-start | bytes 7077892
  603.7 28.9 %copy-start.37 = (f32[1152]{0:T(1024)S(1)}, f32[1152]{0:T(1024)}, u32[]{:S(2)}) copy-start(f32[1152]{0:T(1024)} %copy-done.36) | copy-start | bytes 13828
  632.7 16.2 %copy-start.30 = (bf16[576,72]{0,1:T(8,128)(2,1)S(1)}, bf16[576,72]{0,1:T(8,128)(2,1)}, u32[]{:S(2)}) copy-start(bf16[576,72]{0,1:T(8,128)(2,1)} %reduce-scatter.15.cloned.1.call-done) | copy-start | bytes 248836
  632.7 16.9 %copy-start.27 = (bf16[72,2304]{1,0:T(8,128)(2,1)S(1)}, bf16[72,2304]{1,0:T(8,128)(2,1)}, u32[]{:S(2)}) copy-start(bf16[72,2304]{1,0:T(8,128)(2,1)} %reduce-scatter.11.cloned.1.call-done) | copy-start | bytes 995332
  632.7 17.7 %copy-start.26 = (bf16[2304,72]{0,1:T(8,128)(2,1)S(1)}, bf16[2304,72]{0,1:T(8,128)(2,1)}, u32[]{:S(2)}) copy-start(bf16[2304,72]{0,1:T(8,128)(2,1)} %reduce-scatter.9.cloned.1.call-done) | copy-start | bytes 995332
  636.2 20.0 %copy-start.29 = (f32[16,1152]{1,0:T(8,128)S(1)}, f32[16,1152]{1,0:T(8,128)}, u32[]{:S(2)}) copy-start(f32[16,1152]{1,0:T(8,128)} %copy-done.28) | copy-start | bytes 221188
  636.5 26.6 %copy-start.46 = (bf16[1152]{0:T(1024)(128)(2,1)S(1)}, bf16[1152]{0:T(1024)(128)(2,1)}, u32[]{:S(2)}) copy-start(bf16[1152]{0:T(1024)(128)(2,1)} %copy-done.45) | copy-start | bytes 6916
  647.3 4.3 collective-permute-start.9
  652.7 10.5 %all-to-all-start.2 = ((f32[16,1,576]{2,1,0:T(1,128)}), f32[16,1,576]{2,1,0:T(1,128)S(1)}, u32[]{:S(2)}, u32[]{:S(2)}) async-start(f32[16,1,576]{2,1,0:T(1,128)} %copy.52), calls=%async_computation.4 | async-start | bytes 81920 | tf_op jit(solution)/shard_map/all_to_all | solution.py:96
  (24 other events, 60.1 us)
Sparse Core Ops, SparseCore 0:
  10.2 54.8 all-gather.4
  67.3 37.8 all-gather.6
  107.4 55.2 all-gather.8
  164.7 54.9 all-gather.10
  331.2 57.1 reduce-scatter.14
  392.3 78.6 reduce-scatter.8
  474.9 78.6 reduce-scatter.10
  591.9 71.7 reduce-scatter.12
